TPU v7x, 32 devices: a whole 2x2x4 slice. The times are simulated.
32 devices in a mesh: lon: 4 (over y, x), lat: 8 (over z, core).
Axes of the slice: x: 2, y: 2, z: 4, core: 2. Of those that a mesh axis runs over, the one named last changes fastest.
Arguments:
- wind_east: float32 [16, 64, 2048], P(None, 'lat', 'lon'), may hold values from -6 to 6
- wind_north: float32 [16, 64, 2048], P(None, 'lat', 'lon'), may hold values from -6 to 6
- potential_temp: float32 [16, 64, 2048], P(None, 'lat', 'lon'), may hold values from -6 to 6
- pressure: float32 [16, 64, 2048], P(None, 'lat', 'lon'), may hold values from -6 to 6
- moisture: float32 [16, 64, 2048], P(None, 'lat', 'lon'), may hold values from -6 to 6
- map_factor: float32 [64], P('lat'), may hold values from 1 to 4
- filter_rows: int32 [32], replicated, may hold values from 0 to 63, as said below
- filter_cutoff: int32 [32], replicated, may hold values from 1 to 1025, as said below
Outputs:
- new_east: float32 [16, 64, 2048], P(None, 'lat', 'lon')
- new_north: float32 [16, 64, 2048], P(None, 'lat', 'lon')
- new_temp: float32 [16, 64, 2048], P(None, 'lat', 'lon')
- new_pressure: float32 [16, 64, 2048], P(None, 'lat', 'lon')
- new_moisture: float32 [16, 64, 2048], P(None, 'lat', 'lon')
Inputs may be any that keep to these rules, and one draw needn't show every extreme that they name: `filter_rows`: ascending and without repeats; the rows are the first m and the last 32 - m latitude rows, for some m with 1 <= m <= 31. `filter_cutoff`: within each polar cap the count does not fall with the row's distance from the nearer pole; the row farthest from the pole in each cap keeps 1025.
All inputs are finite; a program needn't handle non-finite values.
Results may differ from a plain program's by a relative error of at most 0.000073.
Values sent between devices are 32-bit elements; how exact they have to be, the bound alone decides.
No kernel may reach another device: no remote copies, remote signals or barrier semaphores. Data moves between devices by JAX's collectives and lax.ppermute only.
A program may use at most 128 MiB of HBM per device.

v0:
```python
import math
import jax
import jax.numpy as jnp
from jax import lax
from jax.sharding import PartitionSpec as P

SUBSTEPS = 4
ADV_COEF = 0.1
SOUND = 0.4
THETA_DIV = 0.3


def extended_2(array, sides, width, wrap):
    for axis, dim in sides:
        devices, length = (lax.axis_size(axis), array.shape[dim])
        up = [(i, (i + 1) % devices) for i in range(devices if wrap else devices - 1)]
        down = [(j, i) for i, j in up]
        last = lax.slice_in_dim(array, length - width, length, axis=dim)
        initial = lax.slice_in_dim(array, 0, width, axis=dim)
        before = lax.ppermute(last, axis, up)
        after = lax.ppermute(initial, axis, down)
        array = jnp.concatenate([before, array, after], axis=dim)
    return array


def centred(shifted):
    return (
        shifted[0]
        - 9.0 * shifted[1]
        + 45.0 * shifted[2]
        - 45.0 * shifted[3]
        + 9.0 * shifted[4]
        - shifted[5]
    ) / 60.0


def damping(shifted, centre):
    return (
        shifted[0]
        - 6.0 * shifted[1]
        + 15.0 * shifted[2]
        - 20.0 * centre
        + 15.0 * shifted[3]
        - 6.0 * shifted[4]
        + shifted[5]
    ) / 60.0


def wave_table(circle):
    half = circle // 2
    points = jnp.arange(circle, dtype=jnp.int32)
    cos_waves = jnp.arange(half + 1, dtype=jnp.int32)
    sin_waves = jnp.arange(1, half, dtype=jnp.int32)
    cos_angles = (points[:, None] * cos_waves[None, :] % circle).astype(jnp.float32) * (
        2.0 * math.pi / circle
    )
    sin_angles = (points[:, None] * sin_waves[None, :] % circle).astype(jnp.float32) * (
        2.0 * math.pi / circle
    )
    table = jnp.concatenate([jnp.cos(cos_angles), jnp.sin(sin_angles)], axis=1)
    wave_index = jnp.concatenate([cos_waves, sin_waves])
    return (table, wave_index)


def filter_circles(circles, table, wave_index, item_cut, flagged, circle):
    spectra = jnp.dot(circles, table, precision=lax.Precision.HIGHEST)
    single = (wave_index == 0) | (wave_index == circle // 2)
    weights = jnp.where(single, 1.0, 2.0) / circle
    kept_mask = wave_index[None, :] < item_cut[:, None]
    spectra = jnp.where(kept_mask, spectra * weights[None, :], 0.0)
    smooth = lax.dot_general(
        spectra, table, (((1,), (1,)), ((), ())), precision=lax.Precision.HIGHEST
    )
    return jnp.where(flagged[:, None], smooth, circles)


def item_tables(item_rows, row_cut, row_flag, rows_dev):
    picked = item_rows[:, None] == jnp.arange(rows_dev, dtype=jnp.int32)[None, :]
    item_cut = jnp.sum(jnp.where(picked, row_cut[None, :], 0), axis=1)
    flagged = jnp.any(picked & row_flag[None, :], axis=1)
    return (item_cut, flagged)


def pole_mask(extended, lat_place, rows_dev, total_rows, depth, row_dim):
    ext_rows = lat_place * rows_dev - depth + jnp.arange(rows_dev + 2 * depth, dtype=jnp.int32)
    inside = (ext_rows >= 0) & (ext_rows < total_rows)
    shape_mask = [1] * extended.ndim
    shape_mask[row_dim] = rows_dev + 2 * depth
    return jnp.where(inside.reshape(shape_mask), extended, 0.0)


def shards(
    wind_east,
    wind_north,
    potential_temp,
    pressure,
    moisture,
    map_factor,
    filter_rows,
    filter_cutoff,
):
    levels, rows_dev, cols_dev = wind_east.shape
    lon_count = lax.axis_size("lon")
    lat_count = lax.axis_size("lat")
    lon_place = lax.axis_index("lon")
    lat_place = lax.axis_index("lat")
    circle = cols_dev * lon_count
    total_rows = rows_dev * lat_count
    local_rows = lat_place * rows_dev + jnp.arange(rows_dev, dtype=jnp.int32)
    matches = filter_rows[:, None] == local_rows[None, :]
    row_flag = jnp.any(matches, axis=0)
    row_cut = jnp.sum(jnp.where(matches, filter_cutoff[:, None], 0), axis=0)
    table, wave_index = wave_table(circle)
    stacked = jnp.stack([wind_east, wind_north, potential_temp, pressure, moisture])
    per_dev = levels * rows_dev // lon_count
    item_ids = lon_place * per_dev + jnp.arange(per_dev, dtype=jnp.int32)
    item_cut, flagged = item_tables(item_ids % rows_dev, row_cut, row_flag, rows_dev)
    results = []
    for field_index in range(5):
        blocks = stacked[field_index].reshape(lon_count, per_dev, cols_dev)
        circles = lax.all_to_all(blocks, "lon", split_axis=0, concat_axis=2, tiled=True)[0]
        smooth = filter_circles(circles, table, wave_index, item_cut, flagged, circle)
        returned = lax.all_to_all(smooth[None], "lon", split_axis=2, concat_axis=0, tiled=True)
        results.append(returned.reshape(levels, rows_dev, cols_dev))
    stacked = jnp.stack(results)
    extended = extended_2(stacked, (("lon", 3), ("lat", 2)), 3, True)
    extended = pole_mask(extended, lat_place, rows_dev, total_rows, 3, 2)
    along = [
        extended[:, :, 3 : 3 + rows_dev, 3 + offset : 3 + offset + cols_dev]
        for offset in (3, 2, 1, -1, -2, -3)
    ]
    across = [
        extended[:, :, 3 + offset : 3 + offset + rows_dev, 3 : 3 + cols_dev]
        for offset in (3, 2, 1, -1, -2, -3)
    ]
    east_wind = stacked[0]
    north_wind = stacked[1]
    coef_x = (ADV_COEF * map_factor)[:, None]
    zonal = east_wind[None] * centred(along) - jnp.abs(east_wind[None]) * damping(along, stacked)
    meridional = north_wind[None] * centred(across) - jnp.abs(north_wind[None]) * damping(
        across, stacked
    )
    tendency = -coef_x * zonal - ADV_COEF * meridional
    tend_east, tend_north, tend_temp, tend_press, tend_moist = (
        tendency[0],
        tendency[1],
        tendency[2],
        tendency[3],
        tendency[4],
    )
    theta_now = stacked[2]
    press_now = stacked[3]
    moist_now = stacked[4]
    grad_x = (SOUND * map_factor)[:, None]
    latitude = -0.5 * math.pi + (local_rows.astype(jnp.float32) + 0.5) * (math.pi / total_rows)
    coriolis = (0.5 * jnp.sin(latitude))[:, None]
    substep_dt = 1.0 / SUBSTEPS
    for substep in range(SUBSTEPS):
        press_ext = extended_2(press_now, (("lon", 2), ("lat", 1)), 1, True)
        press_ext = pole_mask(press_ext, lat_place, rows_dev, total_rows, 1, 1)
        press_dx = (press_ext[:, 1:-1, 2:] - press_ext[:, 1:-1, :-2]) * 0.5
        press_dy = (press_ext[:, 2:, 1:-1] - press_ext[:, :-2, 1:-1]) * 0.5
        east_wind = east_wind + substep_dt * (tend_east - grad_x * press_dx + coriolis * north_wind)
        north_wind = north_wind + substep_dt * (
            tend_north - SOUND * press_dy - coriolis * east_wind
        )
        east_ext = extended_2(east_wind, (("lon", 2),), 1, True)
        north_ext = extended_2(north_wind, (("lat", 1),), 1, False)
        diverge = (
            grad_x * (east_ext[:, :, 2:] - east_ext[:, :, :-2]) * 0.5
            + SOUND * (north_ext[:, 2:, :] - north_ext[:, :-2, :]) * 0.5
        )
        press_now = press_now + substep_dt * (tend_press - diverge)
        theta_now = theta_now + substep_dt * (tend_temp - THETA_DIV * diverge)
        moist_now = moist_now + substep_dt * tend_moist
    return (east_wind, north_wind, theta_now, press_now, moist_now)


def solution(mesh):
    in_specs = (
        P(None, "lat", "lon"),
        P(None, "lat", "lon"),
        P(None, "lat", "lon"),
        P(None, "lat", "lon"),
        P(None, "lat", "lon"),
        P("lat"),
        P(),
        P(),
    )
    out_specs = (
        P(None, "lat", "lon"),
        P(None, "lat", "lon"),
        P(None, "lat", "lon"),
        P(None, "lat", "lon"),
        P(None, "lat", "lon"),
    )
    return jax.shard_map(shards, mesh=mesh, in_specs=in_specs, out_specs=out_specs, check_vma=False)
```

profile of v0, /device:TPU:0, one launch (start us, length us, event | category | flops | bytes accessed | tf_op | source)
XLA Modules:
  0.0 494.1 jit_solution(3201918005113495006)
XLA Ops:
  0.6 5.2 %all-to-all-start = ((f32[4,32,512]{2,1,0:T(8,128)}), f32[4,32,512]{2,1,0:T(8,128)S(1)}, u32[]{:S(2)}, u32[]{:S(2)}) async-start(f32[4,32,512]{2,1,0:T(8,128)} %bitcast.201), calls=%async_computation | async-start | bytes 524288 | tf_op jit(solution)/shard_map/all_to_all | solution.py:121
  5.9 35.4 %fusion.3 = f32[2048,1025]{1,0:T(8,128)} fusion(), kind=kLoop, calls=%fused_computation.10 | loop fusion | flops 29388800 | bytes 8396800 | tf_op jit(solution)/shard_map/cos | solution.py:60
  41.7 32.0 %fusion.10 = f32[2048,1023]{1,0:T(8,128)} fusion(s32[1023]{0:T(1024)S(1)} %iota_add_fusion), kind=kLoop, calls=%fused_computation.17 | loop fusion | flops 29331456 | bytes 8384508 | tf_op jit(solution)/shard_map/sin | solution.py:60
  73.9 4.2 all-to-all-start.4
  78.2 5.3 %all-to-all-done.4 = f32[4,32,512]{2,1,0:T(8,128)S(1)} async-done(((f32[4,32,512]{2,1,0:T(8,128)}), f32[4,32,512]{2,1,0:T(8,128)S(1)}, u32[]{:S(2)}, u32[]{:S(2)}) %all-to-all-start.4) | async-done | bytes 262176 | tf_op jit(solution)/shard_map/all_to_all | solution.py:121
  83.5 3.4 all-to-all-start.8
  87.5 4.8 all-to-all-done.8
  92.2 3.7 all-to-all-start.6
  96.3 17.9 %fusion.26 = f32[32,2048]{1,0:T(8,128)} fusion(f32[32,2048]{1,0:T(8,128)S(1)} %bitcast.182, f32[2048]{0:T(1024)S(1)} %get-tuple-element.18, s32[2048]{0:T(1024)S(1)} %get-tuple-element.19, s32[32]{0:T(128)S(1)} %select_reduce_fusion, f32[2048,1023]{1,0:T(8,128)} %fusion.10, f32[2048,1025]{1,0:T(8,128)} %fusion.3), kind=kOutput, calls=%fused_computation.44 | convolution fusion | flops 1615003648 | bytes 17318016 | tf_op jit(solution)/shard_map/dot_general | solution.py:66
  114.2 15.2 %fusion.28 = f32[32,2048]{1,0:T(8,128)} fusion(f32[32,2048]{1,0:T(8,128)S(1)} %bitcast.184, f32[2048]{0:T(1024)S(1)} %get-tuple-element.18, s32[2048]{0:T(1024)S(1)} %get-tuple-element.19, s32[32]{0:T(128)S(1)} %select_reduce_fusion, f32[2048,1023]{1,0:T(8,128)} %fusion.10, f32[2048,1025]{1,0:T(8,128)S(1)} %bitcast.148), kind=kOutput, calls=%fused_computation.46 | convolution fusion | flops 1615003648 | bytes 17318016 | tf_op jit(solution)/shard_map/dot_general | solution.py:66
  129.4 16.1 %fusion.18 = f32[1,32,2048]{2,1,0:T(8,128)S(1)} fusion(f32[32,2048]{1,0:T(8,128)S(1)} %bitcast.183, f32[32,2048]{1,0:T(8,128)} %fusion.26, pred[32]{0:T(512)(128)(4,1)S(1)} %fusion.96, f32[2048,1023]{1,0:T(8,128)S(1)} %bitcast.150, f32[2048,1025]{1,0:T(8,128)S(1)} %bitcast.148), kind=kOutput, calls=%fused_computation.31 | convolution fusion | flops 1614872576 | bytes 17563680 | tf_op jit(solution)/shard_map/dot_general | solution.py:71
  145.5 16.3 %fusion.14 = f32[1,32,2048]{2,1,0:T(8,128)S(1)} fusion(f32[32,2048]{1,0:T(8,128)S(1)} %bitcast.185, f32[32,2048]{1,0:T(8,128)} %fusion.28, pred[32]{0:T(512)(128)(4,1)S(1)} %fusion.96, f32[2048,1023]{1,0:T(8,128)S(1)} %bitcast.150, f32[2048,1025]{1,0:T(8,128)S(1)} %bitcast.148), kind=kOutput, calls=%fused_computation.23 | convolution fusion | flops 1614872576 | bytes 17563680 | tf_op jit(solution)/shard_map/dot_general | solution.py:71
  161.8 11.5 %fusion.24 = f32[32,2048]{1,0:T(8,128)} fusion(f32[32,2048]{1,0:T(8,128)S(1)} %bitcast.178, f32[2048]{0:T(1024)S(1)} %get-tuple-element.18, s32[2048]{0:T(1024)S(1)} %get-tuple-element.19, s32[32]{0:T(128)S(1)} %select_reduce_fusion, f32[2048,1023]{1,0:T(8,128)S(1)} %bitcast.150, f32[2048,1025]{1,0:T(8,128)S(1)} %bitcast.148), kind=kOutput, calls=%fused_computation.42 | convolution fusion | flops 1615003648 | bytes 17318016 | tf_op jit(solution)/shard_map/dot_general | solution.py:66
  173.3 4.6 all-to-all-start.2
  177.9 20.0 %fusion.22 = f32[1,32,2048]{2,1,0:T(8,128)S(1)} fusion(f32[32,2048]{1,0:T(8,128)S(1)} %bitcast.179, f32[32,2048]{1,0:T(8,128)} %fusion.24, pred[32]{0:T(512)(128)(4,1)S(1)} %fusion.96, f32[2048,1023]{1,0:T(8,128)} %fusion.10, f32[2048,1025]{1,0:T(8,128)} %fusion.3), kind=kOutput, calls=%fused_computation.39 | convolution fusion | flops 1614872576 | bytes 17563680 | tf_op jit(solution)/shard_map/dot_general | solution.py:71
  199.2 9.3 %reduce.4 = f32[2048,32]{1,0:T(8,128)S(1)} reduce(f32[2048,1,32]{2,1,0:T(1,128)S(1)} %bitcast.156, f32[]{:T(128)} %broadcast.311), dimensions={1}, to_apply=%bitcast.123.reduce_sub_computation | reduce | bytes 524292
  210.4 4.4 all-to-all-start.1
  214.8 15.9 %fusion.27 = f32[32,2048]{1,0:T(8,128)} fusion(f32[32,2048]{1,0:T(8,128)S(1)} %bitcast.180, f32[2048]{0:T(1024)S(1)} %get-tuple-element.18, s32[2048]{0:T(1024)S(1)} %get-tuple-element.19, s32[32]{0:T(128)S(1)} %select_reduce_fusion, f32[2048,1023]{1,0:T(8,128)} %fusion.10, f32[2048,1025]{1,0:T(8,128)} %fusion.3), kind=kOutput, calls=%fused_computation.45 | convolution fusion | flops 1615003648 | bytes 17318016 | tf_op jit(solution)/shard_map/dot_general | solution.py:66
  231.2 9.3 %reduce.8 = f32[2048,32]{1,0:T(8,128)S(1)} reduce(f32[2048,1,32]{2,1,0:T(1,128)S(1)} %bitcast.157, f32[]{:T(128)} %broadcast.311), dimensions={1}, to_apply=%bitcast.131.reduce_sub_computation | reduce | bytes 524292
  241.8 4.4 all-to-all-start.9
  246.2 20.0 %fusion.16 = f32[1,32,2048]{2,1,0:T(8,128)S(1)} fusion(f32[32,2048]{1,0:T(8,128)S(1)} %bitcast.181, f32[32,2048]{1,0:T(8,128)} %fusion.27, pred[32]{0:T(512)(128)(4,1)S(1)} %fusion.96, f32[2048,1023]{1,0:T(8,128)} %fusion.10, f32[2048,1025]{1,0:T(8,128)} %fusion.3), kind=kOutput, calls=%fused_computation.27 | convolution fusion | flops 1614872576 | bytes 17563680 | tf_op jit(solution)/shard_map/dot_general | solution.py:71
  267.0 9.3 %reduce.2 = f32[2048,32]{1,0:T(8,128)S(1)} reduce(f32[2048,1,32]{2,1,0:T(1,128)S(1)} %bitcast.158, f32[]{:T(128)} %broadcast.311), dimensions={1}, to_apply=%bitcast.125.reduce_sub_computation | reduce | bytes 524292
  277.6 4.6 all-to-all-start.7
  282.2 15.9 %fusion.25 = f32[32,2048]{1,0:T(8,128)} fusion(f32[32,2048]{1,0:T(8,128)S(1)} %bitcast.176, f32[2048]{0:T(1024)S(1)} %get-tuple-element.18, s32[2048]{0:T(1024)S(1)} %get-tuple-element.19, s32[32]{0:T(128)S(1)} %select_reduce_fusion, f32[2048,1023]{1,0:T(8,128)} %fusion.10, f32[2048,1025]{1,0:T(8,128)} %fusion.3), kind=kOutput, calls=%fused_computation.43 | convolution fusion | flops 1615003648 | bytes 17318016 | tf_op jit(solution)/shard_map/dot_general | solution.py:66
  298.6 9.3 %reduce.6 = f32[2048,32]{1,0:T(8,128)S(1)} reduce(f32[2048,1,32]{2,1,0:T(1,128)S(1)} %bitcast.159, f32[]{:T(128)} %broadcast.311), dimensions={1}, to_apply=%bitcast.129.reduce_sub_computation | reduce | bytes 524292
  309.1 4.4 all-to-all-start.5
  313.5 20.0 %fusion.20 = f32[1,32,2048]{2,1,0:T(8,128)S(1)} fusion(f32[32,2048]{1,0:T(8,128)S(1)} %bitcast.177, f32[32,2048]{1,0:T(8,128)} %fusion.25, pred[32]{0:T(512)(128)(4,1)S(1)} %fusion.96, f32[2048,1023]{1,0:T(8,128)} %fusion.10, f32[2048,1025]{1,0:T(8,128)} %fusion.3), kind=kOutput, calls=%fused_computation.35 | convolution fusion | flops 1614872576 | bytes 17563680 | tf_op jit(solution)/shard_map/dot_general | solution.py:71
  334.0 9.6 %reduce = f32[2048,32]{1,0:T(8,128)S(1)} reduce(f32[2048,1,32]{2,1,0:T(1,128)S(1)} %bitcast.160, f32[]{:T(128)} %broadcast.311), dimensions={1}, to_apply=%bitcast.127.reduce_sub_computation | reduce | bytes 524292
  346.1 1.6 reshape.129
  354.9 4.2 all-to-all-start.3
  359.2 2.0 collective-permute-start.4
  370.8 1.9 collective-permute-start.1
  373.0 3.5 collective-permute-start.7
  377.7 4.0 collective-permute-done.1
  383.6 12.2 %collective-permute-done.3 = f32[5,16,3,518]{3,1,2,0:T(8,128)S(1)} collective-permute-done((f32[5,16,3,518]{3,1,2,0:T(8,128)S(1)}, f32[5,16,3,518]{3,1,2,0:T(8,128)S(1)}, u32[]{:S(2)}, u32[]{:S(2)}) %collective-permute-start.3) | collective-permute-done | bytes 497312 | tf_op jit(solution)/shard_map/ppermute | solution.py:21
  396.2 4.4 collective-permute-done.2
  402.3 4.2 multiply_subtract_fusion
  408.2 3.2 collective-permute-start.11
  413.5 2.7 collective-permute-done.8
  418.2 2.4 collective-permute-start.13
  420.5 2.2 collective-permute-done.12
  423.8 3.5 collective-permute-start.15
  427.4 2.1 collective-permute-done.14
  431.4 3.0 collective-permute-start.19
  434.5 2.2 collective-permute-start.16
  436.9 2.2 collective-permute-done.16
  439.1 2.9 collective-permute-done.17
  442.8 2.5 collective-permute-start.21
  445.3 2.2 collective-permute-done.20
  448.5 3.5 collective-permute-start.23
  452.1 1.7 collective-permute-done.22
  455.7 3.0 collective-permute-start.27
  458.9 2.2 collective-permute-start.24
  461.2 2.2 collective-permute-done.24
  463.4 2.9 collective-permute-done.25
  467.8 2.5 collective-permute-start.29
  470.3 2.2 collective-permute-done.28
  473.6 3.5 collective-permute-start.31
  477.1 1.7 collective-permute-done.30
  480.8 3.0 collective-permute-start.35
  483.9 2.2 collective-permute-start.32
  486.2 2.2 collective-permute-done.32
  488.4 2.9 collective-permute-done.33
  492.3 1.6 multiply_add_fusion.1
  (169 shorter events, 53.8 us)
Async XLA Ops:
  0.6 73.3 %all-to-all-start = ((f32[4,32,512]{2,1,0:T(8,128)}), f32[4,32,512]{2,1,0:T(8,128)S(1)}, u32[]{:S(2)}, u32[]{:S(2)}) async-start(f32[4,32,512]{2,1,0:T(8,128)} %bitcast.201), calls=%async_computation | async-start | bytes 524288 | tf_op jit(solution)/shard_map/all_to_all | solution.py:121
  5.9 35.5 %copy-start.5 = (s32[32]{0:T(128)S(1)}, s32[32]{0:T(128)}, u32[]{:S(2)}) copy-start(s32[32]{0:T(128)} %param.14) | copy-start | bytes 388
  5.9 35.6 %copy-start.4 = (s32[32]{0:T(128)S(1)}, s32[32]{0:T(128)}, u32[]{:S(2)}) copy-start(s32[32]{0:T(128)} %param.15) | copy-start | bytes 388
  41.7 45.2 %copy-start.6 = (f32[8]{0:T(128)S(1)}, f32[8]{0:T(128)}, u32[]{:S(2)}) copy-start(f32[8]{0:T(128)} %param.13) | copy-start | bytes 100
  73.9 9.6 %all-to-all-start.4 = ((f32[4,32,512]{2,1,0:T(8,128)}), f32[4,32,512]{2,1,0:T(8,128)S(1)}, u32[]{:S(2)}, u32[]{:S(2)}) async-start(f32[4,32,512]{2,1,0:T(8,128)} %bitcast.17), calls=%async_computation.4 | async-start | bytes 524288 | tf_op jit(solution)/shard_map/all_to_all | solution.py:121
  83.5 8.8 %all-to-all-start.8 = ((f32[4,32,512]{2,1,0:T(8,128)}), f32[4,32,512]{2,1,0:T(8,128)S(1)}, u32[]{:S(2)}, u32[]{:S(2)}) async-start(f32[4,32,512]{2,1,0:T(8,128)} %bitcast.33), calls=%async_computation.8 | async-start | bytes 524288 | tf_op jit(solution)/shard_map/all_to_all | solution.py:121
  92.2 81.1 %all-to-all-start.6 = ((f32[4,32,512]{2,1,0:T(8,128)}), f32[4,32,512]{2,1,0:T(8,128)S(1)}, u32[]{:S(2)}, u32[]{:S(2)}) async-start(f32[4,32,512]{2,1,0:T(8,128)} %bitcast.25), calls=%async_computation.6 | async-start | bytes 524288 | tf_op jit(solution)/shard_map/all_to_all | solution.py:121
  96.1 18.0 %slice-start = ((s8[9437184]{0:T(1024)(128)(4,1)}), s8[4194304]{0:T(1024)(128)(4,1)S(1)}, s32[]{:S(2)}) async-start(s8[9437184]{0:T(1024)(128)(4,1)} %bitcast.147), calls=%async_computation.10 | async-start | bytes 8388608
  96.2 17.9 %slice-start.1 = ((s8[9437184]{0:T(1024)(128)(4,1)}), s8[4194304]{0:T(1024)(128)(4,1)S(1)}, s32[]{:S(2)}) async-start(s8[9437184]{0:T(1024)(128)(4,1)} %bitcast.147), calls=%async_computation.11 | async-start | bytes 8388608
  96.2 17.9 %slice-start.2 = ((s8[9437184]{0:T(1024)(128)(4,1)}), s8[1048576]{0:T(1024)(128)(4,1)S(1)}, s32[]{:S(2)}) async-start(s8[9437184]{0:T(1024)(128)(4,1)} %bitcast.147), calls=%async_computation.12 | async-start | bytes 2097152
  96.3 33.1 %slice-start.3 = ((s8[8388608]{0:T(1024)(128)(4,1)}), s8[4194304]{0:T(1024)(128)(4,1)S(1)}, s32[]{:S(2)}) async-start(s8[8388608]{0:T(1024)(128)(4,1)} %bitcast.149), calls=%async_computation.13 | async-start | bytes 8388608
  114.2 15.2 %slice-start.4 = ((s8[8388608]{0:T(1024)(128)(4,1)}), s8[4194304]{0:T(1024)(128)(4,1)S(1)}, s32[]{:S(2)}) async-start(s8[8388608]{0:T(1024)(128)(4,1)} %bitcast.149), calls=%async_computation.14 | async-start | bytes 8388608
  173.3 36.4 %all-to-all-start.2 = ((f32[4,32,512]{2,1,0:T(8,128)}), f32[4,32,512]{2,1,0:T(8,128)S(1)}, u32[]{:S(2)}, u32[]{:S(2)}) async-start(f32[4,32,512]{2,1,0:T(8,128)} %bitcast.202), calls=%async_computation.2 | async-start | bytes 524288 | tf_op jit(solution)/shard_map/all_to_all | solution.py:121
  209.7 0.7 copy-start.2
  210.4 31.3 %all-to-all-start.1 = ((f32[4,1,16384]{2,1,0:T(1,128)}), f32[4,1,16384]{2,1,0:T(1,128)S(1)}, u32[]{:S(2)}, u32[]{:S(2)}) async-start(f32[4,1,16384]{2,1,0:T(1,128)} %reshape.128), calls=%async_computation.1 | async-start | bytes 524288 | tf_op jit(solution)/shard_map/all_to_all | solution.py:123
  241.8 35.8 %all-to-all-start.9 = ((f32[4,1,16384]{2,1,0:T(1,128)}), f32[4,1,16384]{2,1,0:T(1,128)S(1)}, u32[]{:S(2)}, u32[]{:S(2)}) async-start(f32[4,1,16384]{2,1,0:T(1,128)} %reshape.136), calls=%async_computation.9 | async-start | bytes 524288 | tf_op jit(solution)/shard_map/all_to_all | solution.py:123
  246.2 20.0 %copy-start.3 = (f32[4,32,512]{2,1,0:T(8,128)S(1)}, f32[4,32,512]{2,1,0:T(8,128)}, u32[]{:S(2)}) copy-start(f32[4,32,512]{2,1,0:T(8,128)} %copy-done.2) | copy-start | bytes 786436
  277.6 31.5 %all-to-all-start.7 = ((f32[4,1,16384]{2,1,0:T(1,128)}), f32[4,1,16384]{2,1,0:T(1,128)S(1)}, u32[]{:S(2)}, u32[]{:S(2)}) async-start(f32[4,1,16384]{2,1,0:T(1,128)} %reshape.130), calls=%async_computation.7 | async-start | bytes 524288 | tf_op jit(solution)/shard_map/all_to_all | solution.py:123
  309.1 45.8 %all-to-all-start.5 = ((f32[4,1,16384]{2,1,0:T(1,128)}), f32[4,1,16384]{2,1,0:T(1,128)S(1)}, u32[]{:S(2)}, u32[]{:S(2)}) async-start(f32[4,1,16384]{2,1,0:T(1,128)} %reshape.134), calls=%async_computation.5 | async-start | bytes 524288 | tf_op jit(solution)/shard_map/all_to_all | solution.py:123
  354.9 11.1 %all-to-all-start.3 = ((f32[4,1,16384]{2,1,0:T(1,128)}), f32[4,1,16384]{2,1,0:T(1,128)S(1)}, u32[]{:S(2)}, u32[]{:S(2)}) async-start(f32[4,1,16384]{2,1,0:T(1,128)} %reshape.132), calls=%async_computation.3 | async-start | bytes 524288 | tf_op jit(solution)/shard_map/all_to_all | solution.py:123
  359.2 13.5 %collective-permute-start.4 = (f32[16,8,1]{2,1,0:T(8,128)S(1)}, f32[16,8,1]{2,1,0:T(8,128)S(1)}, u32[]{:S(2)}, u32[]{:S(2)}) collective-permute-start(f32[16,8,1]{2,1,0:T(8,128)S(1)} %get-tuple-element.60), channel_id=1, source_target_pairs={{0,8},{8,16},{16,24},{24,0},{1,9},{9,17},{17,25},{25,1},{2,10},{10... | collective-permute-start | bytes 1544 | tf_op jit(solution)/shard_map/ppermute | solution.py:20
  361.2 11.4 %collective-permute-start.5 = (f32[16,8,1]{2,1,0:T(8,128)S(1)}, f32[16,8,1]{2,1,0:T(8,128)S(1)}, u32[]{:S(2)}, u32[]{:S(2)}) collective-permute-start(f32[16,8,1]{2,1,0:T(8,128)S(1)} %get-tuple-element.61), channel_id=1, source_target_pairs={{8,0},{16,8},{24,16},{0,24},{9,1},{17,9},{25,17},{1,25},{10,2},{18... | collective-permute-start | bytes 1544 | tf_op jit(solution)/shard_map/ppermute | solution.py:21
  369.7 8.0 %collective-permute-start = (f32[5,16,8,3]{3,2,1,0:T(8,128)S(1)}, f32[5,16,8,3]{3,2,1,0:T(8,128)S(1)}, u32[]{:S(2)}, u32[]{:S(2)}) collective-permute-start(f32[5,16,8,3]{3,2,1,0:T(8,128)S(1)} %get-tuple-element.24), channel_id=1, source_target_pairs={{0,8},{8,16},{16,24},{24,0},{1,9},{9,17},{17,25},{25,1},{2,10},{10... | collective-permute-start | bytes 23048 | tf_op jit(solution)/shard_map/ppermute | solution.py:20
  370.8 10.9 %collective-permute-start.1 = (f32[5,16,8,3]{3,2,1,0:T(8,128)S(1)}, f32[5,16,8,3]{3,2,1,0:T(8,128)S(1)}, u32[]{:S(2)}, u32[]{:S(2)}) collective-permute-start(f32[5,16,8,3]{3,2,1,0:T(8,128)S(1)} %get-tuple-element.25), channel_id=1, source_target_pairs={{8,0},{16,8},{24,16},{0,24},{9,1},{17,9},{25,17},{1,25},{10,2},{18... | collective-permute-start | bytes 23048 | tf_op jit(solution)/shard_map/ppermute | solution.py:21
  372.9 10.4 %collective-permute-start.6 = (f32[16,1,514]{2,1,0:T(1,128)S(1)}, f32[16,1,514]{2,1,0:T(1,128)S(1)}, u32[]{:S(2)}, u32[]{:S(2)}) collective-permute-start(f32[16,1,514]{2,1,0:T(1,128)S(1)} %get-tuple-element.32), channel_id=1, source_target_pairs={{0,1},{1,2},{2,3},{3,4},{4,5},{5,6},{6,7},{7,0},{8,9},{9,10},{10,1... | collective-permute-start | bytes 98696 | tf_op jit(solution)/shard_map/ppermute | solution.py:20
  373.0 10.3 %collective-permute-start.7 = (f32[16,1,514]{2,1,0:T(1,128)S(1)}, f32[16,1,514]{2,1,0:T(1,128)S(1)}, u32[]{:S(2)}, u32[]{:S(2)}) collective-permute-start(f32[16,1,514]{2,1,0:T(1,128)S(1)} %get-tuple-element.33), channel_id=1, source_target_pairs={{1,0},{2,1},{3,2},{4,3},{5,4},{6,5},{7,6},{0,7},{9,8},{10,9},{11,1... | collective-permute-start | bytes 98696 | tf_op jit(solution)/shard_map/ppermute | solution.py:21
  382.6 13.2 %collective-permute-start.3 = (f32[5,16,3,518]{3,1,2,0:T(8,128)S(1)}, f32[5,16,3,518]{3,1,2,0:T(8,128)S(1)}, u32[]{:S(2)}, u32[]{:S(2)}) collective-permute-start(f32[5,16,3,518]{3,1,2,0:T(8,128)S(1)} %copy.108), channel_id=1, source_target_pairs={{1,0},{2,1},{3,2},{4,3},{5,4},{6,5},{7,6},{0,7},{9,8},{10,9},{11,1... | collective-permute-start | bytes 1491848 | tf_op jit(solution)/shard_map/ppermute | solution.py:21
  382.7 17.9 %collective-permute-start.2 = (f32[5,16,3,518]{3,1,2,0:T(8,128)S(1)}, f32[5,16,3,518]{3,1,2,0:T(8,128)S(1)}, u32[]{:S(2)}, u32[]{:S(2)}) collective-permute-start(f32[5,16,3,518]{3,1,2,0:T(8,128)S(1)} %copy.107), channel_id=1, source_target_pairs={{0,1},{1,2},{2,3},{3,4},{4,5},{5,6},{6,7},{7,0},{8,9},{9,10},{10,1... | collective-permute-start | bytes 1491848 | tf_op jit(solution)/shard_map/ppermute | solution.py:20
  406.9 10.3 %collective-permute-start.10 = (f32[16,1,512]{2,1,0:T(1,128)S(1)}, f32[16,1,512]{2,1,0:T(1,128)S(1)}, u32[]{:S(2)}, u32[]{:S(2)}) collective-permute-start(f32[16,1,512]{2,1,0:T(1,128)S(1)} %get-tuple-element.54), channel_id=1, source_target_pairs={{1,0},{2,1},{3,2},{4,3},{5,4},{6,5},{7,6},{9,8},{10,9},{11,10},{12... | collective-permute-start | bytes 98312 | tf_op jit(solution)/shard_map/ppermute | solution.py:21
  408.2 9.1 %collective-permute-start.11 = (f32[16,1,512]{2,1,0:T(1,128)S(1)}, f32[16,1,512]{2,1,0:T(1,128)S(1)}, u32[]{:S(2)}, u32[]{:S(2)}) collective-permute-start(f32[16,1,512]{2,1,0:T(1,128)S(1)} %get-tuple-element.55), channel_id=1, source_target_pairs={{0,1},{1,2},{2,3},{3,4},{4,5},{5,6},{6,7},{8,9},{9,10},{10,11},{11... | collective-permute-start | bytes 98312 | tf_op jit(solution)/shard_map/ppermute | solution.py:20
  411.5 4.8 collective-permute-start.8
  412.1 5.2 %collective-permute-start.9 = (f32[16,8,1]{2,1,0:T(8,128)S(1)}, f32[16,8,1]{2,1,0:T(8,128)S(1)}, u32[]{:S(2)}, u32[]{:S(2)}) collective-permute-start(f32[16,8,1]{2,1,0:T(8,128)S(1)} %get-tuple-element.53), channel_id=1, source_target_pairs={{0,8},{8,16},{16,24},{24,0},{1,9},{9,17},{17,25},{25,1},{2,10},{10... | collective-permute-start | bytes 1544 | tf_op jit(solution)/shard_map/ppermute | solution.py:20
  417.6 5.2 %collective-permute-start.12 = (f32[16,8,1]{2,1,0:T(8,128)S(1)}, f32[16,8,1]{2,1,0:T(8,128)S(1)}, u32[]{:S(2)}, u32[]{:S(2)}) collective-permute-start(f32[16,8,1]{2,1,0:T(8,128)S(1)} %get-tuple-element.50), channel_id=1, source_target_pairs={{0,8},{8,16},{16,24},{24,0},{1,9},{9,17},{17,25},{25,1},{2,10},{10... | collective-permute-start | bytes 1544 | tf_op jit(solution)/shard_map/ppermute | solution.py:20
  418.2 5.3 %collective-permute-start.13 = (f32[16,8,1]{2,1,0:T(8,128)S(1)}, f32[16,8,1]{2,1,0:T(8,128)S(1)}, u32[]{:S(2)}, u32[]{:S(2)}) collective-permute-start(f32[16,8,1]{2,1,0:T(8,128)S(1)} %get-tuple-element.51), channel_id=1, source_target_pairs={{8,0},{16,8},{24,16},{0,24},{9,1},{17,9},{25,17},{1,25},{10,2},{18... | collective-permute-start | bytes 1544 | tf_op jit(solution)/shard_map/ppermute | solution.py:21
  423.8 5.7 %collective-permute-start.14 = (f32[16,1,514]{2,1,0:T(1,128)S(1)}, f32[16,1,514]{2,1,0:T(1,128)S(1)}, u32[]{:S(2)}, u32[]{:S(2)}) collective-permute-start(f32[16,1,514]{2,1,0:T(1,128)S(1)} %get-tuple-element.30), channel_id=1, source_target_pairs={{0,1},{1,2},{2,3},{3,4},{4,5},{5,6},{6,7},{7,0},{8,9},{9,10},{10,1... | collective-permute-start | bytes 98696 | tf_op jit(solution)/shard_map/ppermute | solution.py:20
  423.8 5.6 %collective-permute-start.15 = (f32[16,1,514]{2,1,0:T(1,128)S(1)}, f32[16,1,514]{2,1,0:T(1,128)S(1)}, u32[]{:S(2)}, u32[]{:S(2)}) collective-permute-start(f32[16,1,514]{2,1,0:T(1,128)S(1)} %get-tuple-element.31), channel_id=1, source_target_pairs={{1,0},{2,1},{3,2},{4,3},{5,4},{6,5},{7,6},{0,7},{9,8},{10,9},{11,1... | collective-permute-start | bytes 98696 | tf_op jit(solution)/shard_map/ppermute | solution.py:21
  430.1 11.8 %collective-permute-start.18 = (f32[16,1,512]{2,1,0:T(1,128)S(1)}, f32[16,1,512]{2,1,0:T(1,128)S(1)}, u32[]{:S(2)}, u32[]{:S(2)}) collective-permute-start(f32[16,1,512]{2,1,0:T(1,128)S(1)} %get-tuple-element.48), channel_id=1, source_target_pairs={{1,0},{2,1},{3,2},{4,3},{5,4},{6,5},{7,6},{9,8},{10,9},{11,10},{12... | collective-permute-start | bytes 98312 | tf_op jit(solution)/shard_map/ppermute | solution.py:21
  431.4 10.5 %collective-permute-start.19 = (f32[16,1,512]{2,1,0:T(1,128)S(1)}, f32[16,1,512]{2,1,0:T(1,128)S(1)}, u32[]{:S(2)}, u32[]{:S(2)}) collective-permute-start(f32[16,1,512]{2,1,0:T(1,128)S(1)} %get-tuple-element.49), channel_id=1, source_target_pairs={{0,1},{1,2},{2,3},{3,4},{4,5},{5,6},{6,7},{8,9},{9,10},{10,11},{11... | collective-permute-start | bytes 98312 | tf_op jit(solution)/shard_map/ppermute | solution.py:20
  434.5 4.5 collective-permute-start.16
  436.8 5.2 %collective-permute-start.17 = (f32[16,8,1]{2,1,0:T(8,128)S(1)}, f32[16,8,1]{2,1,0:T(8,128)S(1)}, u32[]{:S(2)}, u32[]{:S(2)}) collective-permute-start(f32[16,8,1]{2,1,0:T(8,128)S(1)} %get-tuple-element.47), channel_id=1, source_target_pairs={{0,8},{8,16},{16,24},{24,0},{1,9},{9,17},{17,25},{25,1},{2,10},{10... | collective-permute-start | bytes 1544 | tf_op jit(solution)/shard_map/ppermute | solution.py:20
  442.3 5.2 %collective-permute-start.20 = (f32[16,8,1]{2,1,0:T(8,128)S(1)}, f32[16,8,1]{2,1,0:T(8,128)S(1)}, u32[]{:S(2)}, u32[]{:S(2)}) collective-permute-start(f32[16,8,1]{2,1,0:T(8,128)S(1)} %get-tuple-element.44), channel_id=1, source_target_pairs={{0,8},{8,16},{16,24},{24,0},{1,9},{9,17},{17,25},{25,1},{2,10},{10... | collective-permute-start | bytes 1544 | tf_op jit(solution)/shard_map/ppermute | solution.py:20
  442.8 5.4 %collective-permute-start.21 = (f32[16,8,1]{2,1,0:T(8,128)S(1)}, f32[16,8,1]{2,1,0:T(8,128)S(1)}, u32[]{:S(2)}, u32[]{:S(2)}) collective-permute-start(f32[16,8,1]{2,1,0:T(8,128)S(1)} %get-tuple-element.45), channel_id=1, source_target_pairs={{8,0},{16,8},{24,16},{0,24},{9,1},{17,9},{25,17},{1,25},{10,2},{18... | collective-permute-start | bytes 1544 | tf_op jit(solution)/shard_map/ppermute | solution.py:21
  448.5 5.3 %collective-permute-start.22 = (f32[16,1,514]{2,1,0:T(1,128)S(1)}, f32[16,1,514]{2,1,0:T(1,128)S(1)}, u32[]{:S(2)}, u32[]{:S(2)}) collective-permute-start(f32[16,1,514]{2,1,0:T(1,128)S(1)} %get-tuple-element.28), channel_id=1, source_target_pairs={{0,1},{1,2},{2,3},{3,4},{4,5},{5,6},{6,7},{7,0},{8,9},{9,10},{10,1... | collective-permute-start | bytes 98696 | tf_op jit(solution)/shard_map/ppermute | solution.py:20
  448.5 5.2 %collective-permute-start.23 = (f32[16,1,514]{2,1,0:T(1,128)S(1)}, f32[16,1,514]{2,1,0:T(1,128)S(1)}, u32[]{:S(2)}, u32[]{:S(2)}) collective-permute-start(f32[16,1,514]{2,1,0:T(1,128)S(1)} %get-tuple-element.29), channel_id=1, source_target_pairs={{1,0},{2,1},{3,2},{4,3},{5,4},{6,5},{7,6},{0,7},{9,8},{10,9},{11,1... | collective-permute-start | bytes 98696 | tf_op jit(solution)/shard_map/ppermute | solution.py:21
  454.4 11.8 %collective-permute-start.26 = (f32[16,1,512]{2,1,0:T(1,128)S(1)}, f32[16,1,512]{2,1,0:T(1,128)S(1)}, u32[]{:S(2)}, u32[]{:S(2)}) collective-permute-start(f32[16,1,512]{2,1,0:T(1,128)S(1)} %get-tuple-element.42), channel_id=1, source_target_pairs={{1,0},{2,1},{3,2},{4,3},{5,4},{6,5},{7,6},{9,8},{10,9},{11,10},{12... | collective-permute-start | bytes 98312 | tf_op jit(solution)/shard_map/ppermute | solution.py:21
  455.7 10.5 %collective-permute-start.27 = (f32[16,1,512]{2,1,0:T(1,128)S(1)}, f32[16,1,512]{2,1,0:T(1,128)S(1)}, u32[]{:S(2)}, u32[]{:S(2)}) collective-permute-start(f32[16,1,512]{2,1,0:T(1,128)S(1)} %get-tuple-element.43), channel_id=1, source_target_pairs={{0,1},{1,2},{2,3},{3,4},{4,5},{5,6},{6,7},{8,9},{9,10},{10,11},{11... | collective-permute-start | bytes 98312 | tf_op jit(solution)/shard_map/ppermute | solution.py:20
  458.9 4.5 collective-permute-start.24
  461.1 5.2 %collective-permute-start.25 = (f32[16,8,1]{2,1,0:T(8,128)S(1)}, f32[16,8,1]{2,1,0:T(8,128)S(1)}, u32[]{:S(2)}, u32[]{:S(2)}) collective-permute-start(f32[16,8,1]{2,1,0:T(8,128)S(1)} %get-tuple-element.41), channel_id=1, source_target_pairs={{0,8},{8,16},{16,24},{24,0},{1,9},{9,17},{17,25},{25,1},{2,10},{10... | collective-permute-start | bytes 1544 | tf_op jit(solution)/shard_map/ppermute | solution.py:20
  467.3 5.2 %collective-permute-start.28 = (f32[16,8,1]{2,1,0:T(8,128)S(1)}, f32[16,8,1]{2,1,0:T(8,128)S(1)}, u32[]{:S(2)}, u32[]{:S(2)}) collective-permute-start(f32[16,8,1]{2,1,0:T(8,128)S(1)} %get-tuple-element.38), channel_id=1, source_target_pairs={{0,8},{8,16},{16,24},{24,0},{1,9},{9,17},{17,25},{25,1},{2,10},{10... | collective-permute-start | bytes 1544 | tf_op jit(solution)/shard_map/ppermute | solution.py:20
  467.8 5.4 %collective-permute-start.29 = (f32[16,8,1]{2,1,0:T(8,128)S(1)}, f32[16,8,1]{2,1,0:T(8,128)S(1)}, u32[]{:S(2)}, u32[]{:S(2)}) collective-permute-start(f32[16,8,1]{2,1,0:T(8,128)S(1)} %get-tuple-element.39), channel_id=1, source_target_pairs={{8,0},{16,8},{24,16},{0,24},{9,1},{17,9},{25,17},{1,25},{10,2},{18... | collective-permute-start | bytes 1544 | tf_op jit(solution)/shard_map/ppermute | solution.py:21
  473.5 5.3 %collective-permute-start.30 = (f32[16,1,514]{2,1,0:T(1,128)S(1)}, f32[16,1,514]{2,1,0:T(1,128)S(1)}, u32[]{:S(2)}, u32[]{:S(2)}) collective-permute-start(f32[16,1,514]{2,1,0:T(1,128)S(1)} %get-tuple-element.26), channel_id=1, source_target_pairs={{0,1},{1,2},{2,3},{3,4},{4,5},{5,6},{6,7},{7,0},{8,9},{9,10},{10,1... | collective-permute-start | bytes 98696 | tf_op jit(solution)/shard_map/ppermute | solution.py:20
  473.6 5.2 %collective-permute-start.31 = (f32[16,1,514]{2,1,0:T(1,128)S(1)}, f32[16,1,514]{2,1,0:T(1,128)S(1)}, u32[]{:S(2)}, u32[]{:S(2)}) collective-permute-start(f32[16,1,514]{2,1,0:T(1,128)S(1)} %get-tuple-element.27), channel_id=1, source_target_pairs={{1,0},{2,1},{3,2},{4,3},{5,4},{6,5},{7,6},{0,7},{9,8},{10,9},{11,1... | collective-permute-start | bytes 98696 | tf_op jit(solution)/shard_map/ppermute | solution.py:21
  479.4 14.4 %copy-start = (f32[16,8,512]{2,1,0:T(8,128)}, f32[16,8,512]{2,1,0:T(8,128)S(1)}, u32[]{:S(2)}) copy-start(f32[16,8,512]{2,1,0:T(8,128)S(1)} %get-tuple-element.11) | copy-start | bytes 786436
  479.4 14.4 %copy-start.1 = (f32[16,8,512]{2,1,0:T(8,128)}, f32[16,8,512]{2,1,0:T(8,128)S(1)}, u32[]{:S(2)}) copy-start(f32[16,8,512]{2,1,0:T(8,128)S(1)} %get-tuple-element.10) | copy-start | bytes 786436
  479.5 11.8 %collective-permute-start.34 = (f32[16,1,512]{2,1,0:T(1,128)S(1)}, f32[16,1,512]{2,1,0:T(1,128)S(1)}, u32[]{:S(2)}, u32[]{:S(2)}) collective-permute-start(f32[16,1,512]{2,1,0:T(1,128)S(1)} %get-tuple-element.36), channel_id=1, source_target_pairs={{1,0},{2,1},{3,2},{4,3},{5,4},{6,5},{7,6},{9,8},{10,9},{11,10},{12... | collective-permute-start | bytes 98312 | tf_op jit(solution)/shard_map/ppermute | solution.py:21
  480.8 10.5 %collective-permute-start.35 = (f32[16,1,512]{2,1,0:T(1,128)S(1)}, f32[16,1,512]{2,1,0:T(1,128)S(1)}, u32[]{:S(2)}, u32[]{:S(2)}) collective-permute-start(f32[16,1,512]{2,1,0:T(1,128)S(1)} %get-tuple-element.37), channel_id=1, source_target_pairs={{0,1},{1,2},{2,3},{3,4},{4,5},{5,6},{6,7},{8,9},{9,10},{10,11},{11... | collective-permute-start | bytes 98312 | tf_op jit(solution)/shard_map/ppermute | solution.py:20
  483.9 4.5 collective-permute-start.32
  486.2 5.2 %collective-permute-start.33 = (f32[16,8,1]{2,1,0:T(8,128)S(1)}, f32[16,8,1]{2,1,0:T(8,128)S(1)}, u32[]{:S(2)}, u32[]{:S(2)}) collective-permute-start(f32[16,8,1]{2,1,0:T(8,128)S(1)} %get-tuple-element.35), channel_id=1, source_target_pairs={{0,8},{8,16},{16,24},{24,0},{1,9},{9,17},{17,25},{25,1},{2,10},{10... | collective-permute-start | bytes 1544 | tf_op jit(solution)/shard_map/ppermute | solution.py:20
where the time goes:
time: 500 us; the launch traced here: 494 us
  matrix products  169 us (34%)
  other arithmetic  136 us (27%)
  starting transfers between devices  99.5 us (20%)
  waiting for transfers between devices  65.2 us (13%)
  local copies, waits for them, and re-layouts  23.2 us (5%)
    dot_general x5, matrix products, filter_circles(): lax.dot_general(spectra, table, (((1,), (1,)), ((), ())), precision=lax.P...  92.3 us
    dot_general x5, matrix products, filter_circles(): spectra = jnp.dot(circles, table, precision=lax.Precision.HIGHEST)  76.2 us
    unnamed x7, other arithmetic  46.9 us
    ppermute x18, starting transfers between devices, extended_2(): after = lax.ppermute(initial, axis, down)  37.2 us
    cos x1, other arithmetic, wave_table(): table = jnp.concatenate([jnp.cos(cos_angles), jnp.sin(sin_angles)], axis=1)  35.4 us
    sin x1, other arithmetic, wave_table(): table = jnp.concatenate([jnp.cos(cos_angles), jnp.sin(sin_angles)], axis=1)  32 us
    ppermute x18, waiting for transfers between devices, extended_2(): after = lax.ppermute(initial, axis, down)  27.7 us
    ppermute x18, waiting for transfers between devices, extended_2(): before = lax.ppermute(last, axis, up)  27.5 us
  transfers between devices with their start and end apart: 46, of which 23 were waited for; matrix products, arithmetic and copies ran while one was open for 63% of the time, Pallas kernels for 0%

commit v1 on v0

--- a/solution.py
+++ b/solution.py
@@ -8,6 +8,18 @@
 ADV_COEF = 0.1
 SOUND = 0.4
 THETA_DIV = 0.3
+
+
+def in_blocks(x, dim, length):
+    dims = x.shape
+    tiles = x.reshape(*dims[:dim], length, dims[dim] // length, *dims[dim + 1 :])
+    return jnp.moveaxis(tiles, dim, 0)
+
+
+def in_order(pieces, dim):
+    pieces = jnp.moveaxis(pieces, 0, dim)
+    dims = pieces.shape
+    return pieces.reshape(*dims[:dim], dims[dim] * dims[dim + 1], *dims[dim + 2 :])
 
 
 def extended_2(array, sides, width, wrap):
@@ -120,7 +132,14 @@
         blocks = stacked[field_index].reshape(lon_count, per_dev, cols_dev)
         circles = lax.all_to_all(blocks, "lon", split_axis=0, concat_axis=2, tiled=True)[0]
         smooth = filter_circles(circles, table, wave_index, item_cut, flagged, circle)
-        returned = lax.all_to_all(smooth[None], "lon", split_axis=2, concat_axis=0, tiled=True)
+        size, mine = (lax.axis_size("lon"), lax.axis_index("lon"))
+        pieces = in_blocks(smooth[None], 2, size)
+        finished = [pieces[mine]]
+        for step in range(1, size):
+            sent = pieces[mine ^ step]
+            finished.append(lax.ppermute(sent, "lon", [(i_2, i_2 ^ step) for i_2 in range(size)]))
+        pieces = jnp.stack(finished)[mine ^ jnp.arange(size)]
+        returned = in_order(pieces, 0)
         results.append(returned.reshape(levels, rows_dev, cols_dev))
     stacked = jnp.stack(results)
     extended = extended_2(stacked, (("lon", 3), ("lat", 2)), 3, True)

time: 500 us -> 429 us (0.86)
  other arithmetic: 136 us -> 80.6 us
  waiting for transfers between devices: 65.2 us -> 53.9 us
  local copies, waits for them, and re-layouts: 23.2 us -> 14.7 us
    unnamed x7 -> x4, other arithmetic: 46.9 us -> 0.01 us
    all_to_all x5 -> x0, starting transfers between devices: 21.9 us -> none  [shards(): lax.all_to_all(smooth[None], 'lon', split_axis=2, concat_axis=0, tiled=True)]
    ppermute x0 -> x15, starting transfers between devices: none -> 20.6 us  [shards(): lax.ppermute(sent, 'lon', [(i_2, i_2 ^ step) for i_2 in range(size)])]
    ppermute x18, waiting for transfers between devices: 27.7 us -> 11.6 us  [extended_2(): after = lax.ppermute(initial, axis, down)]
    unnamed x44 -> x78, local copies, waits for them, and re-layouts: 15.4 us -> 6.83 us
    all_to_all x5 -> x0, other arithmetic: 6.86 us -> none  [shards(): lax.all_to_all(smooth[None], 'lon', split_axis=2, concat_axis=0, tiled=True)]
    ppermute x18, waiting for transfers between devices: 27.5 us -> 34.1 us  [extended_2(): before = lax.ppermute(last, axis, up)]
    dot_general x5, matrix products: 76.2 us -> 82.6 us  [filter_circles(): spectra = jnp.dot(circles, table, precision=lax.Precision.HIGHEST)]
  transfers between devices with their start and end apart: 46 -> 56, of which waited for: 23 -> 22; matrix products, arithmetic and copies ran while one was open for 63% -> 60% of each run, Pallas kernels for 0% -> 0%
where the time goes in v1:
time: 429 us; the launch traced here: 424 us
  matrix products  171 us (40%)
  starting transfers between devices  102 us (24%)
  other arithmetic  80.6 us (19%)
  waiting for transfers between devices  53.9 us (13%)
  local copies, waits for them, and re-layouts  14.7 us (3%)
    dot_general x5, matrix products, filter_circles(): lax.dot_general(spectra, table, (((1,), (1,)), ((), ())), precision=lax.P...  88 us
    dot_general x5, matrix products, filter_circles(): spectra = jnp.dot(circles, table, precision=lax.Precision.HIGHEST)  82.6 us
    ppermute x18, starting transfers between devices, extended_2(): after = lax.ppermute(initial, axis, down)  42.8 us
    cos x1, other arithmetic, wave_table(): table = jnp.concatenate([jnp.cos(cos_angles), jnp.sin(sin_angles)], axis=1)  35.4 us
    ppermute x18, waiting for transfers between devices, extended_2(): before = lax.ppermute(last, axis, up)  34.1 us
    sin x1, other arithmetic, wave_table(): table = jnp.concatenate([jnp.cos(cos_angles), jnp.sin(sin_angles)], axis=1)  32 us
    all_to_all x5, starting transfers between devices, shards(): lax.all_to_all(blocks, 'lon', split_axis=0, concat_axis=2, tiled=True)[0]  21.3 us
    ppermute x15, starting transfers between devices, shards(): lax.ppermute(sent, 'lon', [(i_2, i_2 ^ step) for i_2 in range(size)])  20.6 us
  transfers between devices with their start and end apart: 56, of which 22 were waited for; matrix products, arithmetic and copies ran while one was open for 60% of the time, Pallas kernels for 0%

profile of v1, /device:TPU:0, one launch (start us, length us, event | category | flops | bytes accessed | tf_op | source)
XLA Modules:
  0.0 423.9 jit_solution(8936031144528728896)
XLA Ops:
  0.6 5.2 %all-to-all-start.3 = ((f32[4,32,512]{2,1,0:T(8,128)}), f32[4,32,512]{2,1,0:T(8,128)S(1)}, u32[]{:S(2)}, u32[]{:S(2)}) async-start(f32[4,32,512]{2,1,0:T(8,128)} %bitcast.245), calls=%async_computation.3 | async-start | bytes 524288 | tf_op jit(solution)/shard_map/all_to_all | solution.py:133
  5.8 35.4 %fusion.3 = f32[2048,1025]{1,0:T(8,128)} fusion(), kind=kLoop, calls=%fused_computation.15 | loop fusion | flops 29388800 | bytes 8396800 | tf_op jit(solution)/shard_map/cos | solution.py:72
  41.7 32.0 %fusion.10 = f32[2048,1023]{1,0:T(8,128)} fusion(s32[1023]{0:T(1024)S(1)} %iota_add_fusion), kind=kLoop, calls=%fused_computation.22 | loop fusion | flops 29331456 | bytes 8384508 | tf_op jit(solution)/shard_map/sin | solution.py:72
  74.5 4.2 all-to-all-start.4
  79.5 4.6 %all-to-all-done.4 = f32[4,32,512]{2,1,0:T(8,128)S(1)} async-done(((f32[4,32,512]{2,1,0:T(8,128)}), f32[4,32,512]{2,1,0:T(8,128)S(1)}, u32[]{:S(2)}, u32[]{:S(2)}) %all-to-all-start.4) | async-done | bytes 262176 | tf_op jit(solution)/shard_map/all_to_all | solution.py:133
  84.1 3.9 all-to-all-start.1
  88.3 17.3 %fusion.22 = f32[32,2048]{1,0:T(8,128)S(1)} fusion(f32[32,2048]{1,0:T(8,128)S(1)} %bitcast.225, f32[2048]{0:T(1024)S(1)} %get-tuple-element.23, s32[2048]{0:T(1024)S(1)} %get-tuple-element.24, s32[32]{0:T(128)S(1)} %select_reduce_fusion, f32[2048,1023]{1,0:T(8,128)} %fusion.10, f32[2048,1025]{1,0:T(8,128)} %fusion.3), kind=kOutput, calls=%fused_computation.45 | convolution fusion | flops 1615003648 | bytes 17318016 | tf_op jit(solution)/shard_map/dot_general | solution.py:78
  105.7 15.5 %fusion.23 = f32[32,2048]{1,0:T(8,128)S(1)} fusion(f32[32,2048]{1,0:T(8,128)S(1)} %bitcast.229, f32[2048]{0:T(1024)} %copy-done, s32[2048]{0:T(1024)} %copy-done.2, s32[32]{0:T(128)} %copy-done.9, f32[2048,1023]{1,0:T(8,128)} %fusion.10, f32[2048,1025]{1,0:T(8,128)S(1)} %bitcast.205), kind=kOutput, calls=%fused_computation.46 | convolution fusion | flops 1615003648 | bytes 17318016 | tf_op jit(solution)/shard_map/dot_general | solution.py:78
  121.2 15.2 %convolution_select_fusion.1 = f32[32,2048]{1,0:T(8,128)S(1)} fusion(f32[32,2048]{1,0:T(8,128)S(1)} %bitcast.226, f32[32,2048]{1,0:T(8,128)S(1)} %fusion.22, pred[32]{0:T(512)(128)(4,1)S(1)} %fusion.94, f32[2048,1023]{1,0:T(8,128)S(1)} %bitcast.211, f32[2048,1025]{1,0:T(8,128)S(1)} %bitcast.205), kind=kOutput, calls=%fused_computation.30 | convolution fusion | flops 1614872576 | bytes 17563680 | tf_op jit(solution)/shard_map/dot_general | solution.py:83
  136.4 15.6 %convolution_select_fusion = f32[32,2048]{1,0:T(8,128)S(1)} fusion(f32[32,2048]{1,0:T(8,128)S(1)} %bitcast.230, f32[32,2048]{1,0:T(8,128)S(1)} %fusion.23, pred[32]{0:T(512)(128)(4,1)S(1)} %fusion.94, f32[2048,1023]{1,0:T(8,128)S(1)} %bitcast.211, f32[2048,1025]{1,0:T(8,128)S(1)} %bitcast.205), kind=kOutput, calls=%fused_computation.27 | convolution fusion | flops 1614872576 | bytes 17563680 | tf_op jit(solution)/shard_map/dot_general | solution.py:83
  153.1 2.1 collective-permute-start.12
  155.2 1.5 collective-permute-start.13
  156.7 3.5 all-to-all-start.2
  160.6 17.3 %fusion.20 = f32[32,2048]{1,0:T(8,128)S(1)} fusion(f32[32,2048]{1,0:T(8,128)S(1)} %bitcast.231, f32[2048]{0:T(1024)S(1)} %copy-done.1, s32[2048]{0:T(1024)S(1)} %copy-done.3, s32[32]{0:T(128)S(1)} %copy-done.10, f32[2048,1023]{1,0:T(8,128)} %fusion.10, f32[2048,1025]{1,0:T(8,128)} %fusion.3), kind=kOutput, calls=%fused_computation.43 | convolution fusion | flops 1615003648 | bytes 17318016 | tf_op jit(solution)/shard_map/dot_general | solution.py:78
  177.9 18.5 %convolution_select_fusion.3 = f32[32,2048]{1,0:T(8,128)S(1)} fusion(f32[32,2048]{1,0:T(8,128)S(1)} %bitcast.232, f32[32,2048]{1,0:T(8,128)S(1)} %fusion.20, pred[32]{0:T(512)(128)(4,1)S(1)} %fusion.94, f32[2048,1023]{1,0:T(8,128)} %fusion.10, f32[2048,1025]{1,0:T(8,128)S(1)} %bitcast.207), kind=kOutput, calls=%fused_computation.36 | convolution fusion | flops 1614872576 | bytes 17563680 | tf_op jit(solution)/shard_map/dot_general | solution.py:83
  196.4 4.6 %all-to-all-start = ((f32[4,32,512]{2,1,0:T(8,128)}), f32[4,32,512]{2,1,0:T(8,128)S(1)}, u32[]{:S(2)}, u32[]{:S(2)}) async-start(f32[4,32,512]{2,1,0:T(8,128)} %bitcast), calls=%async_computation | async-start | bytes 524288 | tf_op jit(solution)/shard_map/all_to_all | solution.py:133
  201.3 15.2 %fusion.21 = f32[32,2048]{1,0:T(8,128)S(1)} fusion(f32[32,2048]{1,0:T(8,128)S(1)} %bitcast.233, f32[2048]{0:T(1024)S(1)} %copy-done.1, s32[2048]{0:T(1024)S(1)} %copy-done.3, s32[32]{0:T(128)S(1)} %copy-done.10, f32[2048,1023]{1,0:T(8,128)} %fusion.10, f32[2048,1025]{1,0:T(8,128)} %fusion.3), kind=kOutput, calls=%fused_computation.44 | convolution fusion | flops 1615003648 | bytes 17318016 | tf_op jit(solution)/shard_map/dot_general | solution.py:78
  216.5 20.1 %convolution_select_fusion.2 = f32[32,2048]{1,0:T(8,128)S(1)} fusion(f32[32,2048]{1,0:T(8,128)S(1)} %bitcast.234, f32[32,2048]{1,0:T(8,128)S(1)} %fusion.21, pred[32]{0:T(512)(128)(4,1)S(1)} %fusion.94, f32[2048,1023]{1,0:T(8,128)} %fusion.10, f32[2048,1025]{1,0:T(8,128)} %fusion.3), kind=kOutput, calls=%fused_computation.33 | convolution fusion | flops 1614872576 | bytes 17563680 | tf_op jit(solution)/shard_map/dot_general | solution.py:83
  237.3 17.3 %fusion.19 = f32[32,2048]{1,0:T(8,128)S(1)} fusion(f32[32,2048]{1,0:T(8,128)S(1)} %bitcast.227, f32[2048]{0:T(1024)S(1)} %copy-done.1, s32[2048]{0:T(1024)S(1)} %copy-done.3, s32[32]{0:T(128)S(1)} %copy-done.10, f32[2048,1023]{1,0:T(8,128)} %fusion.10, f32[2048,1025]{1,0:T(8,128)} %fusion.3), kind=kOutput, calls=%fused_computation.42 | convolution fusion | flops 1615003648 | bytes 17318016 | tf_op jit(solution)/shard_map/dot_general | solution.py:78
  254.6 18.5 %convolution_select_fusion.4 = f32[32,2048]{1,0:T(8,128)S(1)} fusion(f32[32,2048]{1,0:T(8,128)S(1)} %bitcast.228, f32[32,2048]{1,0:T(8,128)S(1)} %fusion.19, pred[32]{0:T(512)(128)(4,1)S(1)} %fusion.94, f32[2048,1023]{1,0:T(8,128)} %fusion.10, f32[2048,1025]{1,0:T(8,128)S(1)} %bitcast.209), kind=kOutput, calls=%fused_computation.39 | convolution fusion | flops 1614872576 | bytes 17563680 | tf_op jit(solution)/shard_map/dot_general | solution.py:83
  273.6 2.1 collective-permute-start
  275.7 1.5 collective-permute-start.1
  279.2 2.9 collective-permute-start.14
  284.6 1.9 collective-permute-start.8
  289.6 1.9 collective-permute-start.5
  293.8 1.9 collective-permute-start.11
  297.1 3.4 collective-permute-done.10
  302.2 2.8 collective-permute-start.16
  305.3 2.9 collective-permute-start.20
  308.2 1.8 collective-permute-done.15
  310.0 3.1 collective-permute-done.16
  313.7 3.5 collective-permute-start.18
  317.4 3.7 collective-permute-start.22
  321.8 8.5 %collective-permute-done.21 = f32[16,1,514]{2,0,1:T(8,128)S(1)} collective-permute-done((f32[16,1,514]{2,0,1:T(8,128)S(1)}, f32[16,1,514]{2,0,1:T(8,128)S(1)}, u32[]{:S(2)}, u32[]{:S(2)}) %collective-permute-start.21) | collective-permute-done | bytes 32928 | tf_op jit(solution)/shard_map/ppermute | solution.py:32
  331.3 4.0 multiply_subtract_fusion
  335.7 1.3 collective-permute-start.25
  337.0 4.5 %collective-permute-start.26 = (f32[16,1,512]{2,0,1:T(8,128)S(1)}, f32[16,1,512]{2,0,1:T(8,128)S(1)}, u32[]{:S(2)}, u32[]{:S(2)}) collective-permute-start(f32[16,1,512]{2,0,1:T(8,128)S(1)} %get-tuple-element.60), channel_id=1, source_target_pairs={{0,1},{1,2},{2,3},{3,4},{4,5},{5,6},{6,7},{8,9},{9,10},{10,11},{11... | collective-permute-start | bytes 98312 | tf_op jit(solution)/shard_map/ppermute | solution.py:32
  342.2 1.5 collective-permute-start.24
  343.7 2.2 collective-permute-done.23
  345.9 2.1 collective-permute-done.24
  348.7 2.7 collective-permute-start.28
  351.4 2.9 collective-permute-done.27
  354.8 3.5 collective-permute-start.30
  358.3 2.2 collective-permute-done.29
  361.0 1.3 collective-permute-start.33
  362.3 3.0 collective-permute-start.34
  365.5 1.6 collective-permute-start.31
  367.5 2.8 collective-permute-done.31
  370.3 2.5 collective-permute-done.32
  373.5 2.6 collective-permute-start.36
  376.1 2.8 collective-permute-done.35
  379.2 3.5 collective-permute-start.38
  382.7 1.9 collective-permute-done.37
  386.4 3.0 collective-permute-start.42
  389.5 2.0 collective-permute-start.39
  391.6 2.5 collective-permute-done.39
  394.1 2.8 collective-permute-done.40
  398.2 2.2 collective-permute-start.44
  400.3 2.3 collective-permute-done.43
  403.1 3.5 collective-permute-start.46
  406.7 1.8 collective-permute-done.45
  410.3 3.0 collective-permute-start.50
  413.4 2.4 collective-permute-start.47
  418.4 2.6 collective-permute-done.48
  (221 shorter events, 35.3 us)
Async XLA Ops:
  0.6 73.9 %all-to-all-start.3 = ((f32[4,32,512]{2,1,0:T(8,128)}), f32[4,32,512]{2,1,0:T(8,128)S(1)}, u32[]{:S(2)}, u32[]{:S(2)}) async-start(f32[4,32,512]{2,1,0:T(8,128)} %bitcast.245), calls=%async_computation.3 | async-start | bytes 524288 | tf_op jit(solution)/shard_map/all_to_all | solution.py:133
  5.8 35.5 %copy-start.7 = (s32[32]{0:T(128)S(1)}, s32[32]{0:T(128)}, u32[]{:S(2)}) copy-start(s32[32]{0:T(128)} %param.14) | copy-start | bytes 388
  5.8 35.7 %copy-start.6 = (s32[32]{0:T(128)S(1)}, s32[32]{0:T(128)}, u32[]{:S(2)}) copy-start(s32[32]{0:T(128)} %param.15) | copy-start | bytes 388
  41.7 37.0 %copy-start.8 = (f32[8]{0:T(128)S(1)}, f32[8]{0:T(128)}, u32[]{:S(2)}) copy-start(f32[8]{0:T(128)} %param.13) | copy-start | bytes 100
  73.8 31.8 %copy-start = (f32[2048]{0:T(1024)}, f32[2048]{0:T(1024)S(1)}, u32[]{:S(2)}) copy-start(f32[2048]{0:T(1024)S(1)} %get-tuple-element.23) | copy-start | bytes 24580
  73.8 31.8 %copy-start.2 = (s32[2048]{0:T(1024)}, s32[2048]{0:T(1024)S(1)}, u32[]{:S(2)}) copy-start(s32[2048]{0:T(1024)S(1)} %get-tuple-element.24) | copy-start | bytes 24580
  74.4 31.2 %copy-start.9 = (s32[32]{0:T(128)}, s32[32]{0:T(128)S(1)}, u32[]{:S(2)}) copy-start(s32[32]{0:T(128)S(1)} %select_reduce_fusion) | copy-start | bytes 388
  74.5 9.6 %all-to-all-start.4 = ((f32[4,32,512]{2,1,0:T(8,128)}), f32[4,32,512]{2,1,0:T(8,128)S(1)}, u32[]{:S(2)}, u32[]{:S(2)}) async-start(f32[4,32,512]{2,1,0:T(8,128)} %bitcast.38), calls=%async_computation.4 | async-start | bytes 524288 | tf_op jit(solution)/shard_map/all_to_all | solution.py:133
  84.1 72.6 %all-to-all-start.1 = ((f32[4,32,512]{2,1,0:T(8,128)}), f32[4,32,512]{2,1,0:T(8,128)S(1)}, u32[]{:S(2)}, u32[]{:S(2)}) async-start(f32[4,32,512]{2,1,0:T(8,128)} %bitcast.11), calls=%async_computation.1 | async-start | bytes 524288 | tf_op jit(solution)/shard_map/all_to_all | solution.py:133
  88.3 32.9 %slice-start.9 = ((s8[8388608]{0:T(1024)(128)(4,1)}), s8[4194304]{0:T(1024)(128)(4,1)S(1)}, s32[]{:S(2)}) async-start(s8[8388608]{0:T(1024)(128)(4,1)} %bitcast.210), calls=%async_computation.14 | async-start | bytes 8388608
  153.1 131.4 %collective-permute-start.12 = (f32[1,32,512]{2,1,0:T(8,128)S(1)}, f32[1,32,512]{2,1,0:T(8,128)}, u32[]{:S(2)}, u32[]{:S(2)}) collective-permute-start(f32[1,32,512]{2,1,0:T(8,128)S(1)} %bitcast.252), channel_id=1, source_target_pairs={{0,8},{8,0},{16,24},{24,16},{1,9},{9,1},{17,25},{25,17},{2,10},{10... | collective-permute-start | bytes 196616 | tf_op jit(solution)/shard_map/ppermute | solution.py:140
  155.2 131.3 %collective-permute-start.13 = (f32[1,32,512]{2,1,0:T(8,128)S(1)}, f32[1,32,512]{2,1,0:T(8,128)}, u32[]{:S(2)}, u32[]{:S(2)}) collective-permute-start(f32[1,32,512]{2,1,0:T(8,128)S(1)} %bitcast.251), channel_id=1, source_target_pairs={{0,16},{8,24},{16,0},{24,8},{1,17},{9,25},{17,1},{25,9},{2,18},{10... | collective-permute-start | bytes 196616 | tf_op jit(solution)/shard_map/ppermute | solution.py:140
  156.7 21.2 %slice-start.3 = ((s8[9437184]{0:T(1024)(128)(4,1)}), s8[1048576]{0:T(1024)(128)(4,1)S(1)}, s32[]{:S(2)}) async-start(s8[9437184]{0:T(1024)(128)(4,1)} %bitcast.206), calls=%async_computation.8 | async-start | bytes 2097152
  156.7 39.7 %all-to-all-start.2 = ((f32[4,32,512]{2,1,0:T(8,128)}), f32[4,32,512]{2,1,0:T(8,128)S(1)}, u32[]{:S(2)}, u32[]{:S(2)}) async-start(f32[4,32,512]{2,1,0:T(8,128)} %bitcast.20), calls=%async_computation.2 | async-start | bytes 524288 | tf_op jit(solution)/shard_map/all_to_all | solution.py:133
  196.4 40.6 %all-to-all-start = ((f32[4,32,512]{2,1,0:T(8,128)}), f32[4,32,512]{2,1,0:T(8,128)S(1)}, u32[]{:S(2)}, u32[]{:S(2)}) async-start(f32[4,32,512]{2,1,0:T(8,128)} %bitcast), calls=%async_computation | async-start | bytes 524288 | tf_op jit(solution)/shard_map/all_to_all | solution.py:133
  273.6 5.6 %collective-permute-start = (f32[1,32,512]{2,1,0:T(8,128)S(1)}, f32[1,32,512]{2,1,0:T(8,128)S(1)}, u32[]{:S(2)}, u32[]{:S(2)}) collective-permute-start(f32[1,32,512]{2,1,0:T(8,128)S(1)} %bitcast.263), channel_id=1, source_target_pairs={{0,8},{8,0},{16,24},{24,16},{1,9},{9,1},{17,25},{25,17},{2,10},{10... | collective-permute-start | bytes 196616 | tf_op jit(solution)/shard_map/ppermute | solution.py:140
  275.7 6.4 %collective-permute-start.1 = (f32[1,32,512]{2,1,0:T(8,128)S(1)}, f32[1,32,512]{2,1,0:T(8,128)S(1)}, u32[]{:S(2)}, u32[]{:S(2)}) collective-permute-start(f32[1,32,512]{2,1,0:T(8,128)S(1)} %bitcast.262), channel_id=1, source_target_pairs={{0,16},{8,24},{16,0},{24,8},{1,17},{9,25},{17,1},{25,9},{2,18},{10... | collective-permute-start | bytes 196616 | tf_op jit(solution)/shard_map/ppermute | solution.py:140
  277.2 5.6 %collective-permute-start.2 = (f32[1,32,512]{2,1,0:T(8,128)S(1)}, f32[1,32,512]{2,1,0:T(8,128)S(1)}, u32[]{:S(2)}, u32[]{:S(2)}) collective-permute-start(f32[1,32,512]{2,1,0:T(8,128)S(1)} %bitcast.261), channel_id=1, source_target_pairs={{0,24},{8,16},{16,8},{24,0},{1,25},{9,17},{17,9},{25,1},{2,26},{10... | collective-permute-start | bytes 196616 | tf_op jit(solution)/shard_map/ppermute | solution.py:140
  279.2 7.9 %collective-permute-start.14 = (f32[1,32,512]{2,1,0:T(8,128)S(1)}, f32[1,32,512]{2,1,0:T(8,128)S(1)}, u32[]{:S(2)}, u32[]{:S(2)}) collective-permute-start(f32[1,32,512]{2,1,0:T(8,128)S(1)} %bitcast.253), channel_id=1, source_target_pairs={{0,24},{8,16},{16,8},{24,0},{1,25},{9,17},{17,9},{25,1},{2,26},{10... | collective-permute-start | bytes 196616 | tf_op jit(solution)/shard_map/ppermute | solution.py:140
  282.1 7.5 %collective-permute-start.6 = (f32[1,32,512]{2,1,0:T(8,128)}, f32[1,32,512]{2,1,0:T(8,128)S(1)}, u32[]{:S(2)}, u32[]{:S(2)}) collective-permute-start(f32[1,32,512]{2,1,0:T(8,128)} %bitcast.194), channel_id=1, source_target_pairs={{0,8},{8,0},{16,24},{24,16},{1,9},{9,1},{17,25},{25,17},{2,10},{10... | collective-permute-start | bytes 196616 | tf_op jit(solution)/shard_map/ppermute | solution.py:140
  282.8 8.7 %collective-permute-start.7 = (f32[1,32,512]{2,1,0:T(8,128)}, f32[1,32,512]{2,1,0:T(8,128)S(1)}, u32[]{:S(2)}, u32[]{:S(2)}) collective-permute-start(f32[1,32,512]{2,1,0:T(8,128)} %bitcast.193), channel_id=1, source_target_pairs={{0,16},{8,24},{16,0},{24,8},{1,17},{9,25},{17,1},{25,9},{2,18},{10... | collective-permute-start | bytes 196616 | tf_op jit(solution)/shard_map/ppermute | solution.py:140
  284.6 7.6 %collective-permute-start.8 = (f32[1,32,512]{2,1,0:T(8,128)S(1)}, f32[1,32,512]{2,1,0:T(8,128)S(1)}, u32[]{:S(2)}, u32[]{:S(2)}) collective-permute-start(f32[1,32,512]{2,1,0:T(8,128)S(1)} %bitcast.260), channel_id=1, source_target_pairs={{0,24},{8,16},{16,8},{24,0},{1,25},{9,17},{17,9},{25,1},{2,26},{10... | collective-permute-start | bytes 196616 | tf_op jit(solution)/shard_map/ppermute | solution.py:140
  286.5 7.3 %collective-permute-start.3 = (f32[1,32,512]{2,1,0:T(8,128)S(1)}, f32[1,32,512]{2,1,0:T(8,128)S(1)}, u32[]{:S(2)}, u32[]{:S(2)}) collective-permute-start(f32[1,32,512]{2,1,0:T(8,128)S(1)} %bitcast.259), channel_id=1, source_target_pairs={{0,8},{8,0},{16,24},{24,16},{1,9},{9,1},{17,25},{25,17},{2,10},{10... | collective-permute-start | bytes 196616 | tf_op jit(solution)/shard_map/ppermute | solution.py:140
  287.1 8.5 %collective-permute-start.4 = (f32[1,32,512]{2,1,0:T(8,128)S(1)}, f32[1,32,512]{2,1,0:T(8,128)S(1)}, u32[]{:S(2)}, u32[]{:S(2)}) collective-permute-start(f32[1,32,512]{2,1,0:T(8,128)S(1)} %bitcast.258), channel_id=1, source_target_pairs={{0,16},{8,24},{16,0},{24,8},{1,17},{9,25},{17,1},{25,9},{2,18},{10... | collective-permute-start | bytes 196616 | tf_op jit(solution)/shard_map/ppermute | solution.py:140
  289.6 6.1 %collective-permute-start.5 = (f32[1,32,512]{2,1,0:T(8,128)S(1)}, f32[1,32,512]{2,1,0:T(8,128)}, u32[]{:S(2)}, u32[]{:S(2)}) collective-permute-start(f32[1,32,512]{2,1,0:T(8,128)S(1)} %bitcast.257), channel_id=1, source_target_pairs={{0,24},{8,16},{16,8},{24,0},{1,25},{9,17},{17,9},{25,1},{2,26},{10... | collective-permute-start | bytes 196616 | tf_op jit(solution)/shard_map/ppermute | solution.py:140
  291.5 5.6 %collective-permute-start.9 = (f32[1,32,512]{2,1,0:T(8,128)S(1)}, f32[1,32,512]{2,1,0:T(8,128)S(1)}, u32[]{:S(2)}, u32[]{:S(2)}) collective-permute-start(f32[1,32,512]{2,1,0:T(8,128)S(1)} %bitcast.256), channel_id=1, source_target_pairs={{0,8},{8,0},{16,24},{24,16},{1,9},{9,1},{17,25},{25,17},{2,10},{10... | collective-permute-start | bytes 196616 | tf_op jit(solution)/shard_map/ppermute | solution.py:140
  292.2 8.4 %collective-permute-start.10 = (f32[1,32,512]{2,1,0:T(8,128)S(1)}, f32[1,32,512]{2,1,0:T(8,128)S(1)}, u32[]{:S(2)}, u32[]{:S(2)}) collective-permute-start(f32[1,32,512]{2,1,0:T(8,128)S(1)} %bitcast.255), channel_id=1, source_target_pairs={{0,16},{8,24},{16,0},{24,8},{1,17},{9,25},{17,1},{25,9},{2,18},{10... | collective-permute-start | bytes 196616 | tf_op jit(solution)/shard_map/ppermute | solution.py:140
  293.8 6.8 %collective-permute-start.11 = (f32[1,32,512]{2,1,0:T(8,128)S(1)}, f32[1,32,512]{2,1,0:T(8,128)S(1)}, u32[]{:S(2)}, u32[]{:S(2)}) collective-permute-start(f32[1,32,512]{2,1,0:T(8,128)S(1)} %bitcast.254), channel_id=1, source_target_pairs={{0,24},{8,16},{16,8},{24,0},{1,25},{9,17},{17,9},{25,1},{2,26},{10... | collective-permute-start | bytes 196616 | tf_op jit(solution)/shard_map/ppermute | solution.py:140
  302.0 8.0 %collective-permute-start.15 = (f32[5,16,8,3]{3,1,2,0:T(8,128)S(1)}, f32[5,16,8,3]{3,1,2,0:T(8,128)S(1)}, u32[]{:S(2)}, u32[]{:S(2)}) collective-permute-start(f32[5,16,8,3]{3,1,2,0:T(8,128)S(1)} %get-tuple-element.29), channel_id=1, source_target_pairs={{0,8},{8,16},{16,24},{24,0},{1,9},{9,17},{17,25},{25,1},{2,10},{10... | collective-permute-start | bytes 23048 | tf_op jit(solution)/shard_map/ppermute | solution.py:32
  302.2 11.0 %collective-permute-start.16 = (f32[5,16,8,3]{3,1,2,0:T(8,128)S(1)}, f32[5,16,8,3]{3,1,2,0:T(8,128)S(1)}, u32[]{:S(2)}, u32[]{:S(2)}) collective-permute-start(f32[5,16,8,3]{3,1,2,0:T(8,128)S(1)} %get-tuple-element.30), channel_id=1, source_target_pairs={{8,0},{16,8},{24,16},{0,24},{9,1},{17,9},{25,17},{1,25},{10,2},{18... | collective-permute-start | bytes 23048 | tf_op jit(solution)/shard_map/ppermute | solution.py:33
  305.3 11.9 %collective-permute-start.19 = (f32[16,8,1]{2,0,1:T(8,128)S(1)}, f32[16,8,1]{2,0,1:T(8,128)S(1)}, u32[]{:S(2)}, u32[]{:S(2)}) collective-permute-start(f32[16,8,1]{2,0,1:T(8,128)S(1)} %get-tuple-element.81), channel_id=1, source_target_pairs={{0,8},{8,16},{16,24},{24,0},{1,9},{9,17},{17,25},{25,1},{2,10},{10... | collective-permute-start | bytes 1544 | tf_op jit(solution)/shard_map/ppermute | solution.py:32
  305.3 11.9 %collective-permute-start.20 = (f32[16,8,1]{2,0,1:T(8,128)S(1)}, f32[16,8,1]{2,0,1:T(8,128)S(1)}, u32[]{:S(2)}, u32[]{:S(2)}) collective-permute-start(f32[16,8,1]{2,0,1:T(8,128)S(1)} %get-tuple-element.82), channel_id=1, source_target_pairs={{8,0},{16,8},{24,16},{0,24},{9,1},{17,9},{25,17},{1,25},{10,2},{18... | collective-permute-start | bytes 1544 | tf_op jit(solution)/shard_map/ppermute | solution.py:33
  313.6 16.9 %collective-permute-start.17 = (f32[5,16,3,518]{3,1,2,0:T(8,128)S(1)}, f32[5,16,3,518]{3,1,2,0:T(8,128)S(1)}, u32[]{:S(2)}, u32[]{:S(2)}) collective-permute-start(f32[5,16,3,518]{3,1,2,0:T(8,128)S(1)} %get-tuple-element.25), channel_id=1, source_target_pairs={{0,1},{1,2},{2,3},{3,4},{4,5},{5,6},{6,7},{7,0},{8,9},{9,10},{10,1... | collective-permute-start | bytes 1491848 | tf_op jit(solution)/shard_map/ppermute | solution.py:32
  313.7 16.9 %collective-permute-start.18 = (f32[5,16,3,518]{3,1,2,0:T(8,128)S(1)}, f32[5,16,3,518]{3,1,2,0:T(8,128)S(1)}, u32[]{:S(2)}, u32[]{:S(2)}) collective-permute-start(f32[5,16,3,518]{3,1,2,0:T(8,128)S(1)} %get-tuple-element.26), channel_id=1, source_target_pairs={{1,0},{2,1},{3,2},{4,3},{5,4},{6,5},{7,6},{0,7},{9,8},{10,9},{11,1... | collective-permute-start | bytes 1491848 | tf_op jit(solution)/shard_map/ppermute | solution.py:33
  317.3 13.0 %collective-permute-start.21 = (f32[16,1,514]{2,0,1:T(8,128)S(1)}, f32[16,1,514]{2,0,1:T(8,128)S(1)}, u32[]{:S(2)}, u32[]{:S(2)}) collective-permute-start(f32[16,1,514]{2,0,1:T(8,128)S(1)} %get-tuple-element.37), channel_id=1, source_target_pairs={{0,1},{1,2},{2,3},{3,4},{4,5},{5,6},{6,7},{7,0},{8,9},{9,10},{10,1... | collective-permute-start | bytes 98696 | tf_op jit(solution)/shard_map/ppermute | solution.py:32
  317.4 13.0 %collective-permute-start.22 = (f32[16,1,514]{2,0,1:T(8,128)S(1)}, f32[16,1,514]{2,0,1:T(8,128)S(1)}, u32[]{:S(2)}, u32[]{:S(2)}) collective-permute-start(f32[16,1,514]{2,0,1:T(8,128)S(1)} %get-tuple-element.38), channel_id=1, source_target_pairs={{1,0},{2,1},{3,2},{4,3},{5,4},{6,5},{7,6},{0,7},{9,8},{10,9},{11,1... | collective-permute-start | bytes 98696 | tf_op jit(solution)/shard_map/ppermute | solution.py:33
  335.7 12.3 %collective-permute-start.25 = (f32[16,1,512]{2,0,1:T(8,128)S(1)}, f32[16,1,512]{2,0,1:T(8,128)S(1)}, u32[]{:S(2)}, u32[]{:S(2)}) collective-permute-start(f32[16,1,512]{2,0,1:T(8,128)S(1)} %get-tuple-element.59), channel_id=1, source_target_pairs={{1,0},{2,1},{3,2},{4,3},{5,4},{6,5},{7,6},{9,8},{10,9},{11,10},{12... | collective-permute-start | bytes 98312 | tf_op jit(solution)/shard_map/ppermute | solution.py:33
  337.0 11.0 %collective-permute-start.26 = (f32[16,1,512]{2,0,1:T(8,128)S(1)}, f32[16,1,512]{2,0,1:T(8,128)S(1)}, u32[]{:S(2)}, u32[]{:S(2)}) collective-permute-start(f32[16,1,512]{2,0,1:T(8,128)S(1)} %get-tuple-element.60), channel_id=1, source_target_pairs={{0,1},{1,2},{2,3},{3,4},{4,5},{5,6},{6,7},{8,9},{9,10},{10,11},{11... | collective-permute-start | bytes 98312 | tf_op jit(solution)/shard_map/ppermute | solution.py:32
  341.6 4.3 %collective-permute-start.23 = (f32[16,8,1]{2,0,1:T(8,128)S(1)}, f32[16,8,1]{2,0,1:T(8,128)S(1)}, u32[]{:S(2)}, u32[]{:S(2)}) collective-permute-start(f32[16,8,1]{2,0,1:T(8,128)S(1)} %get-tuple-element.57), channel_id=1, source_target_pairs={{8,0},{16,8},{24,16},{0,24},{9,1},{17,9},{25,17},{1,25},{10,2},{18... | collective-permute-start | bytes 1544 | tf_op jit(solution)/shard_map/ppermute | solution.py:33
  342.2 5.9 %collective-permute-start.24 = (f32[16,8,1]{2,0,1:T(8,128)S(1)}, f32[16,8,1]{2,0,1:T(8,128)S(1)}, u32[]{:S(2)}, u32[]{:S(2)}) collective-permute-start(f32[16,8,1]{2,0,1:T(8,128)S(1)} %get-tuple-element.58), channel_id=1, source_target_pairs={{0,8},{8,16},{16,24},{24,0},{1,9},{9,17},{17,25},{25,1},{2,10},{10... | collective-permute-start | bytes 1544 | tf_op jit(solution)/shard_map/ppermute | solution.py:32
  348.4 5.8 %collective-permute-start.27 = (f32[16,8,1]{2,0,1:T(8,128)S(1)}, f32[16,8,1]{2,0,1:T(8,128)S(1)}, u32[]{:S(2)}, u32[]{:S(2)}) collective-permute-start(f32[16,8,1]{2,0,1:T(8,128)S(1)} %get-tuple-element.55), channel_id=1, source_target_pairs={{0,8},{8,16},{16,24},{24,0},{1,9},{9,17},{17,25},{25,1},{2,10},{10... | collective-permute-start | bytes 1544 | tf_op jit(solution)/shard_map/ppermute | solution.py:32
  348.7 6.0 %collective-permute-start.28 = (f32[16,8,1]{2,0,1:T(8,128)S(1)}, f32[16,8,1]{2,0,1:T(8,128)S(1)}, u32[]{:S(2)}, u32[]{:S(2)}) collective-permute-start(f32[16,8,1]{2,0,1:T(8,128)S(1)} %get-tuple-element.56), channel_id=1, source_target_pairs={{8,0},{16,8},{24,16},{0,24},{9,1},{17,9},{25,17},{1,25},{10,2},{18... | collective-permute-start | bytes 1544 | tf_op jit(solution)/shard_map/ppermute | solution.py:33
  354.7 5.8 %collective-permute-start.29 = (f32[16,1,514]{2,0,1:T(8,128)S(1)}, f32[16,1,514]{2,0,1:T(8,128)S(1)}, u32[]{:S(2)}, u32[]{:S(2)}) collective-permute-start(f32[16,1,514]{2,0,1:T(8,128)S(1)} %get-tuple-element.35), channel_id=1, source_target_pairs={{0,1},{1,2},{2,3},{3,4},{4,5},{5,6},{6,7},{7,0},{8,9},{9,10},{10,1... | collective-permute-start | bytes 98696 | tf_op jit(solution)/shard_map/ppermute | solution.py:32
  354.8 5.7 %collective-permute-start.30 = (f32[16,1,514]{2,0,1:T(8,128)S(1)}, f32[16,1,514]{2,0,1:T(8,128)S(1)}, u32[]{:S(2)}, u32[]{:S(2)}) collective-permute-start(f32[16,1,514]{2,0,1:T(8,128)S(1)} %get-tuple-element.36), channel_id=1, source_target_pairs={{1,0},{2,1},{3,2},{4,3},{5,4},{6,5},{7,6},{0,7},{9,8},{10,9},{11,1... | collective-permute-start | bytes 98696 | tf_op jit(solution)/shard_map/ppermute | solution.py:33
  361.0 11.8 %collective-permute-start.33 = (f32[16,1,512]{2,0,1:T(8,128)S(1)}, f32[16,1,512]{2,0,1:T(8,128)S(1)}, u32[]{:S(2)}, u32[]{:S(2)}) collective-permute-start(f32[16,1,512]{2,0,1:T(8,128)S(1)} %get-tuple-element.53), channel_id=1, source_target_pairs={{1,0},{2,1},{3,2},{4,3},{5,4},{6,5},{7,6},{9,8},{10,9},{11,10},{12... | collective-permute-start | bytes 98312 | tf_op jit(solution)/shard_map/ppermute | solution.py:33
  362.3 10.5 %collective-permute-start.34 = (f32[16,1,512]{2,0,1:T(8,128)S(1)}, f32[16,1,512]{2,0,1:T(8,128)S(1)}, u32[]{:S(2)}, u32[]{:S(2)}) collective-permute-start(f32[16,1,512]{2,0,1:T(8,128)S(1)} %get-tuple-element.54), channel_id=1, source_target_pairs={{0,1},{1,2},{2,3},{3,4},{4,5},{5,6},{6,7},{8,9},{9,10},{10,11},{11... | collective-permute-start | bytes 98312 | tf_op jit(solution)/shard_map/ppermute | solution.py:32
  365.5 4.9 %collective-permute-start.31 = (f32[16,8,1]{2,0,1:T(8,128)S(1)}, f32[16,8,1]{2,0,1:T(8,128)S(1)}, u32[]{:S(2)}, u32[]{:S(2)}) collective-permute-start(f32[16,8,1]{2,0,1:T(8,128)S(1)} %get-tuple-element.51), channel_id=1, source_target_pairs={{8,0},{16,8},{24,16},{0,24},{9,1},{17,9},{25,17},{1,25},{10,2},{18... | collective-permute-start | bytes 1544 | tf_op jit(solution)/shard_map/ppermute | solution.py:33
  367.0 5.8 %collective-permute-start.32 = (f32[16,8,1]{2,0,1:T(8,128)S(1)}, f32[16,8,1]{2,0,1:T(8,128)S(1)}, u32[]{:S(2)}, u32[]{:S(2)}) collective-permute-start(f32[16,8,1]{2,0,1:T(8,128)S(1)} %get-tuple-element.52), channel_id=1, source_target_pairs={{0,8},{8,16},{16,24},{24,0},{1,9},{9,17},{17,25},{25,1},{2,10},{10... | collective-permute-start | bytes 1544 | tf_op jit(solution)/shard_map/ppermute | solution.py:32
  373.1 5.7 %collective-permute-start.35 = (f32[16,8,1]{2,0,1:T(8,128)S(1)}, f32[16,8,1]{2,0,1:T(8,128)S(1)}, u32[]{:S(2)}, u32[]{:S(2)}) collective-permute-start(f32[16,8,1]{2,0,1:T(8,128)S(1)} %get-tuple-element.49), channel_id=1, source_target_pairs={{0,8},{8,16},{16,24},{24,0},{1,9},{9,17},{17,25},{25,1},{2,10},{10... | collective-permute-start | bytes 1544 | tf_op jit(solution)/shard_map/ppermute | solution.py:32
  373.5 5.6 %collective-permute-start.36 = (f32[16,8,1]{2,0,1:T(8,128)S(1)}, f32[16,8,1]{2,0,1:T(8,128)S(1)}, u32[]{:S(2)}, u32[]{:S(2)}) collective-permute-start(f32[16,8,1]{2,0,1:T(8,128)S(1)} %get-tuple-element.50), channel_id=1, source_target_pairs={{8,0},{16,8},{24,16},{0,24},{9,1},{17,9},{25,17},{1,25},{10,2},{18... | collective-permute-start | bytes 1544 | tf_op jit(solution)/shard_map/ppermute | solution.py:33
  379.1 5.5 %collective-permute-start.37 = (f32[16,1,514]{2,0,1:T(8,128)S(1)}, f32[16,1,514]{2,0,1:T(8,128)S(1)}, u32[]{:S(2)}, u32[]{:S(2)}) collective-permute-start(f32[16,1,514]{2,0,1:T(8,128)S(1)} %get-tuple-element.33), channel_id=1, source_target_pairs={{0,1},{1,2},{2,3},{3,4},{4,5},{5,6},{6,7},{7,0},{8,9},{9,10},{10,1... | collective-permute-start | bytes 98696 | tf_op jit(solution)/shard_map/ppermute | solution.py:32
  379.2 5.4 %collective-permute-start.38 = (f32[16,1,514]{2,0,1:T(8,128)S(1)}, f32[16,1,514]{2,0,1:T(8,128)S(1)}, u32[]{:S(2)}, u32[]{:S(2)}) collective-permute-start(f32[16,1,514]{2,0,1:T(8,128)S(1)} %get-tuple-element.34), channel_id=1, source_target_pairs={{1,0},{2,1},{3,2},{4,3},{5,4},{6,5},{7,6},{0,7},{9,8},{10,9},{11,1... | collective-permute-start | bytes 98696 | tf_op jit(solution)/shard_map/ppermute | solution.py:33
  385.1 11.8 %collective-permute-start.41 = (f32[16,1,512]{2,0,1:T(8,128)S(1)}, f32[16,1,512]{2,0,1:T(8,128)S(1)}, u32[]{:S(2)}, u32[]{:S(2)}) collective-permute-start(f32[16,1,512]{2,0,1:T(8,128)S(1)} %get-tuple-element.47), channel_id=1, source_target_pairs={{1,0},{2,1},{3,2},{4,3},{5,4},{6,5},{7,6},{9,8},{10,9},{11,10},{12... | collective-permute-start | bytes 98312 | tf_op jit(solution)/shard_map/ppermute | solution.py:33
  386.4 10.5 %collective-permute-start.42 = (f32[16,1,512]{2,0,1:T(8,128)S(1)}, f32[16,1,512]{2,0,1:T(8,128)S(1)}, u32[]{:S(2)}, u32[]{:S(2)}) collective-permute-start(f32[16,1,512]{2,0,1:T(8,128)S(1)} %get-tuple-element.48), channel_id=1, source_target_pairs={{0,1},{1,2},{2,3},{3,4},{4,5},{5,6},{6,7},{8,9},{9,10},{10,11},{11... | collective-permute-start | bytes 98312 | tf_op jit(solution)/shard_map/ppermute | solution.py:32
  389.5 4.6 %collective-permute-start.39 = (f32[16,8,1]{2,0,1:T(8,128)S(1)}, f32[16,8,1]{2,0,1:T(8,128)S(1)}, u32[]{:S(2)}, u32[]{:S(2)}) collective-permute-start(f32[16,8,1]{2,0,1:T(8,128)S(1)} %get-tuple-element.45), channel_id=1, source_target_pairs={{8,0},{16,8},{24,16},{0,24},{9,1},{17,9},{25,17},{1,25},{10,2},{18... | collective-permute-start | bytes 1544 | tf_op jit(solution)/shard_map/ppermute | solution.py:33
  391.6 5.3 %collective-permute-start.40 = (f32[16,8,1]{2,0,1:T(8,128)S(1)}, f32[16,8,1]{2,0,1:T(8,128)S(1)}, u32[]{:S(2)}, u32[]{:S(2)}) collective-permute-start(f32[16,8,1]{2,0,1:T(8,128)S(1)} %get-tuple-element.46), channel_id=1, source_target_pairs={{0,8},{8,16},{16,24},{24,0},{1,9},{9,17},{17,25},{25,1},{2,10},{10... | collective-permute-start | bytes 1544 | tf_op jit(solution)/shard_map/ppermute | solution.py:32
  397.4 5.3 %collective-permute-start.43 = (f32[16,8,1]{2,0,1:T(8,128)S(1)}, f32[16,8,1]{2,0,1:T(8,128)S(1)}, u32[]{:S(2)}, u32[]{:S(2)}) collective-permute-start(f32[16,8,1]{2,0,1:T(8,128)S(1)} %get-tuple-element.43), channel_id=1, source_target_pairs={{0,8},{8,16},{16,24},{24,0},{1,9},{9,17},{17,25},{25,1},{2,10},{10... | collective-permute-start | bytes 1544 | tf_op jit(solution)/shard_map/ppermute | solution.py:32
  398.2 4.8 %collective-permute-start.44 = (f32[16,8,1]{2,0,1:T(8,128)S(1)}, f32[16,8,1]{2,0,1:T(8,128)S(1)}, u32[]{:S(2)}, u32[]{:S(2)}) collective-permute-start(f32[16,8,1]{2,0,1:T(8,128)S(1)} %get-tuple-element.44), channel_id=1, source_target_pairs={{8,0},{16,8},{24,16},{0,24},{9,1},{17,9},{25,17},{1,25},{10,2},{18... | collective-permute-start | bytes 1544 | tf_op jit(solution)/shard_map/ppermute | solution.py:33
  403.1 5.4 %collective-permute-start.45 = (f32[16,1,514]{2,0,1:T(8,128)S(1)}, f32[16,1,514]{2,0,1:T(8,128)S(1)}, u32[]{:S(2)}, u32[]{:S(2)}) collective-permute-start(f32[16,1,514]{2,0,1:T(8,128)S(1)} %get-tuple-element.31), channel_id=1, source_target_pairs={{0,1},{1,2},{2,3},{3,4},{4,5},{5,6},{6,7},{7,0},{8,9},{9,10},{10,1... | collective-permute-start | bytes 98696 | tf_op jit(solution)/shard_map/ppermute | solution.py:32
  403.1 5.3 %collective-permute-start.46 = (f32[16,1,514]{2,0,1:T(8,128)S(1)}, f32[16,1,514]{2,0,1:T(8,128)S(1)}, u32[]{:S(2)}, u32[]{:S(2)}) collective-permute-start(f32[16,1,514]{2,0,1:T(8,128)S(1)} %get-tuple-element.32), channel_id=1, source_target_pairs={{1,0},{2,1},{3,2},{4,3},{5,4},{6,5},{7,6},{0,7},{9,8},{10,9},{11,1... | collective-permute-start | bytes 98696 | tf_op jit(solution)/shard_map/ppermute | solution.py:33
  409.0 12.0 %collective-permute-start.49 = (f32[16,1,512]{2,0,1:T(8,128)S(1)}, f32[16,1,512]{2,0,1:T(8,128)S(1)}, u32[]{:S(2)}, u32[]{:S(2)}) collective-permute-start(f32[16,1,512]{2,0,1:T(8,128)S(1)} %get-tuple-element.41), channel_id=1, source_target_pairs={{1,0},{2,1},{3,2},{4,3},{5,4},{6,5},{7,6},{9,8},{10,9},{11,10},{12... | collective-permute-start | bytes 98312 | tf_op jit(solution)/shard_map/ppermute | solution.py:33
  410.3 10.7 %collective-permute-start.50 = (f32[16,1,512]{2,0,1:T(8,128)S(1)}, f32[16,1,512]{2,0,1:T(8,128)S(1)}, u32[]{:S(2)}, u32[]{:S(2)}) collective-permute-start(f32[16,1,512]{2,0,1:T(8,128)S(1)} %get-tuple-element.42), channel_id=1, source_target_pairs={{0,1},{1,2},{2,3},{3,4},{4,5},{5,6},{6,7},{8,9},{9,10},{10,11},{11... | collective-permute-start | bytes 98312 | tf_op jit(solution)/shard_map/ppermute | solution.py:32
  413.4 5.0 %collective-permute-start.47 = (f32[16,8,1]{2,0,1:T(8,128)S(1)}, f32[16,8,1]{2,0,1:T(8,128)S(1)}, u32[]{:S(2)}, u32[]{:S(2)}) collective-permute-start(f32[16,8,1]{2,0,1:T(8,128)S(1)} %get-tuple-element.39), channel_id=1, source_target_pairs={{8,0},{16,8},{24,16},{0,24},{9,1},{17,9},{25,17},{1,25},{10,2},{18... | collective-permute-start | bytes 1544 | tf_op jit(solution)/shard_map/ppermute | solution.py:33
  415.8 5.2 %collective-permute-start.48 = (f32[16,8,1]{2,0,1:T(8,128)S(1)}, f32[16,8,1]{2,0,1:T(8,128)S(1)}, u32[]{:S(2)}, u32[]{:S(2)}) collective-permute-start(f32[16,8,1]{2,0,1:T(8,128)S(1)} %get-tuple-element.40), channel_id=1, source_target_pairs={{0,8},{8,16},{16,24},{24,0},{1,9},{9,17},{17,25},{25,1},{2,10},{10... | collective-permute-start | bytes 1544 | tf_op jit(solution)/shard_map/ppermute | solution.py:32
  (14 other events, 198.3 us)
